TPU v7x, 256 devices: a whole 4x4x8 slice. The times are simulated.
256 devices in a mesh: tm: 16 (over y_lo, x, core), col: 16 (over z, y_hi).
Axes of the slice: x: 4, y: 4 (y_hi: 2, y_lo: 2; y = y_hi * 2 + y_lo), z: 8, core: 2. Of those that a mesh axis runs over, the one named last changes fastest.
Arguments:
- panel: bfloat16 [1024, 131072], P('col', 'tm'), may hold values from -60 to 60
- response: float32 [131072], replicated, may hold values from 0.25 to 2.5
Outputs:
- normal: float32 [1024, 1024], P('col', 'tm')
All inputs are finite; a program needn't handle non-finite values.
Results may differ from a plain program's by a relative error of at most 0.0015.
Values may be sent and summed in bfloat16 or wider, within the bound.
No kernel may reach another device: no remote copies, remote signals or barrier semaphores. Data moves between devices by JAX's collectives and lax.ppermute only.
A program may use at most 64 MiB of HBM per device.

v0:
```python
import math

import jax
import jax.numpy as jnp
from jax import lax
from jax.sharding import PartitionSpec as P

EPOCHS = 131072


def angle_tables(row_count, col_count, length):
    row_index = jnp.arange(row_count, dtype=jnp.int32)[:, None]
    col_index = jnp.arange(col_count, dtype=jnp.int32)[None, :]
    phase_index = row_index * col_index % length
    angle = phase_index.astype(jnp.float32) * (2.0 * math.pi / length)
    return (jnp.cos(angle), jnp.sin(angle))


def mixed(form, left, right):
    return jnp.einsum(form, left, right, precision=lax.Precision.HIGHEST)


def split_table(table):
    upper = table.astype(jnp.bfloat16)
    lower = (table - upper.astype(jnp.float32)).astype(jnp.bfloat16)
    return (upper, lower)


def exact_first(table, values):
    upper, lower = split_table(table)
    first = jnp.einsum("kja,jban->kbn", upper, values, preferred_element_type=jnp.float32)
    return first + jnp.einsum("kja,jban->kbn", lower, values, preferred_element_type=jnp.float32)


def whiten_series(series, tables):
    outer_cos, outer_sin, twist_cos, twist_sin, inner_cos, inner_sin, gain_grid = tables
    block_count, item_count, block_len = series.shape
    inner_len = inner_cos.shape[0]
    steps_per_block = block_len // inner_len
    outer_len = block_count * steps_per_block
    values = series.reshape(block_count, item_count, steps_per_block, inner_len)
    fold_cos = outer_cos.reshape(outer_len, block_count, steps_per_block)
    fold_sin = outer_sin.reshape(outer_len, block_count, steps_per_block)
    first_re = exact_first(fold_cos, values)
    first_im = -exact_first(fold_sin, values)
    turn_cos = twist_cos[:, None, :]
    turn_sin = twist_sin[:, None, :]
    turned_re = first_re * turn_cos + first_im * turn_sin
    turned_im = first_im * turn_cos - first_re * turn_sin
    spec_re = mixed("kbn,nl->kbl", turned_re, inner_cos) + mixed(
        "kbn,nl->kbl", turned_im, inner_sin
    )
    spec_im = mixed("kbn,nl->kbl", turned_im, inner_cos) - mixed(
        "kbn,nl->kbl", turned_re, inner_sin
    )
    weight = gain_grid[:, None, :]
    filt_re = spec_re * weight
    filt_im = spec_im * weight
    back_re = mixed("kbl,ln->kbn", filt_re, inner_cos) - mixed("kbl,ln->kbn", filt_im, inner_sin)
    back_im = mixed("kbl,ln->kbn", filt_im, inner_cos) + mixed("kbl,ln->kbn", filt_re, inner_sin)
    untw_re = back_re * turn_cos - back_im * turn_sin
    untw_im = back_im * turn_cos + back_re * turn_sin
    spread_cos = outer_cos.reshape(block_count, steps_per_block, outer_len)
    spread_sin = outer_sin.reshape(block_count, steps_per_block, outer_len)
    result = mixed("jak,kbn->jban", spread_cos, untw_re) - mixed(
        "jak,kbn->jban", spread_sin, untw_im
    )
    result = result * (1.0 / (outer_len * inner_len))
    return result.reshape(block_count, item_count, block_len).astype(jnp.bfloat16)


def on_device(panel, response):
    col_rows, epoch_count = panel.shape
    tm_count = lax.axis_size("tm")
    total_len = tm_count * epoch_count
    inner_len = math.gcd(256, epoch_count)
    outer_len = total_len // inner_len
    outer_cos, outer_sin = angle_tables(outer_len, outer_len, outer_len)
    twist_cos, twist_sin = angle_tables(outer_len, inner_len, total_len)
    inner_cos, inner_sin = angle_tables(inner_len, inner_len, inner_len)
    gain_grid = response.reshape(inner_len, outer_len).T
    tables = (outer_cos, outer_sin, twist_cos, twist_sin, inner_cos, inner_sin, gain_grid)
    grouped = panel.reshape(tm_count, col_rows // tm_count, epoch_count)
    filtered = whiten_series(
        lax.all_to_all(grouped, "tm", split_axis=0, concat_axis=0, tiled=True), tables
    )
    landed = lax.all_to_all(filtered, "tm", split_axis=0, concat_axis=0, tiled=True)
    whitened = landed.reshape(col_rows, epoch_count)
    partial_sum = lax.dot_general(
        whitened,
        lax.all_gather(whitened, "col", axis=0, tiled=True),
        (((1,), (1,)), ((), ())),
        preferred_element_type=jnp.float32,
    )
    summed = lax.psum_scatter(partial_sum, "tm", scatter_dimension=1, tiled=True)
    return summed / EPOCHS


def solution(mesh):
    in_specs = (P("col", "tm"), P())
    out_specs = P("col", "tm")
    return jax.shard_map(
        on_device, mesh=mesh, in_specs=in_specs, out_specs=out_specs, check_vma=False
    )
```

profile of v0, /device:TPU:8, one launch (start us, length us, event | category | flops | bytes accessed | tf_op | source)
XLA Modules:
  0.0 415.9 jit_solution(12158881425810183495)
XLA Ops:
  6.5 2.3 reshape.89
  8.8 5.8 %all-to-all-start = ((bf16[16,4,8192]{2,1,0:T(4,128)(2,1)}), bf16[16,4,8192]{2,1,0:T(4,128)(2,1)S(1)}, u32[]{:S(2)}, u32[]{:S(2)}) async-start(bf16[16,4,8192]{2,1,0:T(4,128)(2,1)} %reshape.89), calls=%async_computation | async-start | bytes 2097152 | tf_op jit(solution)/shard_map/all_to_all | solution.py:85
  14.6 0.0 all-gather.2.cloned.1.call-start
  14.7 0.1 reshape.91
  14.7 0.2 copy.8
  15.0 2.1 fusion.79
  17.0 12.7 %all-to-all-done = bf16[16,4,8192]{2,1,0:T(4,128)(2,1)S(1)} async-done(((bf16[16,4,8192]{2,1,0:T(4,128)(2,1)}), bf16[16,4,8192]{2,1,0:T(4,128)(2,1)S(1)}, u32[]{:S(2)}, u32[]{:S(2)}) %all-to-all-start) | async-done | bytes 1048608 | tf_op jit(solution)/shard_map/all_to_all | solution.py:85
  29.7 2.0 reshape.107
  31.7 5.7 %fusion.43 = f32[512,4,256,1]{2,0,1,3:T(8,128)S(1)} fusion(bf16[16,4,32,256]{3,2,1,0:T(8,128)(2,1)} %reshape.107, s32[16,32]{1,0:T(8,128)S(1)} %multiply_add_fusion.3), kind=kOutput, calls=%fused_computation.58 | convolution fusion | flops 540803072 | bytes 3147776 | tf_op jit(solution)/shard_map/kja,jban->kbn/dot_general | solution.py:31
  37.4 4.4 %fusion.45 = f32[512,4,256,1]{2,0,1,3:T(8,128)S(1)} fusion(bf16[16,4,32,256]{3,2,1,0:T(8,128)(2,1)S(1)} %copy-done.1, s32[16,32]{1,0:T(8,128)S(1)} %multiply_add_fusion.3), kind=kOutput, calls=%fused_computation.60 | convolution fusion | flops 540803072 | bytes 3147776 | tf_op jit(solution)/shard_map/kja,jban->kbn/dot_general | solution.py:31
  41.8 4.6 %fusion = f32[512,4,256]{2,0,1:T(8,128)S(1)} fusion(f32[512,4,256,1]{2,0,1,3:T(8,128)S(1)} %fusion.43, bf16[16,4,32,256]{3,2,1,0:T(8,128)(2,1)S(1)} %copy-done.1, s32[16,32]{1,0:T(8,128)S(1)} %multiply_add_fusion.3), kind=kOutput, calls=%fused_computation.1 | convolution fusion | flops 542638080 | bytes 5244928 | tf_op jit(solution)/shard_map/kja,jban->kbn/dot_general | solution.py:32
  46.4 4.4 %bitcast_add_fusion.1 = f32[512,4,256]{2,0,1:T(8,128)S(1)} fusion(f32[512,4,256,1]{2,0,1,3:T(8,128)S(1)} %fusion.45, bf16[16,4,32,256]{3,2,1,0:T(8,128)(2,1)S(1)} %copy-done.1, s32[16,32]{1,0:T(8,128)S(1)} %multiply_add_fusion.3), kind=kOutput, calls=%fused_computation.2 | convolution fusion | flops 542113792 | bytes 5244928 | tf_op jit(solution)/shard_map/kja,jban->kbn/dot_general | solution.py:32
  50.8 3.1 fusion.71
  53.9 3.1 fusion.75
  57.0 3.4 subtract_multiply_fusion
  60.4 2.8 fusion.69
  63.2 3.2 add_multiply_fusion
  66.4 2.8 fusion.73
  69.3 3.3 convolution_add_fusion
  72.6 2.9 convolution_subtract_fusion
  75.6 7.8 %fusion.1 = f32[4,256,16,32]{1,3,2,0:T(8,128)S(1)} fusion(f32[512,4,256]{2,0,1:T(8,128)S(1)} %convolution_subtract_fusion, f32[512,4,256]{2,0,1:T(8,128)S(1)} %convolution_add_fusion, f32[512,256]{1,0:T(8,128)S(1)} %get-tuple-element.5, f32[512,256]{1,0:T(8,128)S(1)} %get-tuple-element.6, s32[16,32]{1,0:T(8,128)S(1)} %multiply_add_fusion.3), kind=kOutput, calls=%fused_computation.3 | convolution fusion | flops 3226468352 | bytes 7342080 | tf_op jit(solution)/shard_map/jak,kbn->jban/dot_general | solution.py:20
  83.4 7.7 %fusion.13 = bf16[16,4,32,256]{3,2,0,1:T(8,128)(2,1)S(1)} fusion(f32[4,256,16,32]{1,3,2,0:T(8,128)S(1)} %fusion.1, f32[512,4,256]{2,0,1:T(8,128)S(1)} %convolution_add_fusion, f32[512,4,256]{2,0,1:T(8,128)S(1)} %convolution_subtract_fusion, f32[512,256]{1,0:T(8,128)S(1)} %get-tuple-element.5, f32[512,256]{1,0:T(8,128)S(1)} %get-tuple-element.6, ...), kind=kOutput, calls=%fused_computation.26 | convolution fusion | flops 3228041216 | bytes 8390656 | tf_op jit(solution)/shard_map/jak,kbn->jban/dot_general | solution.py:20
  91.1 0.5 convert_element_type.101
  91.6 0.8 copy.9
  92.5 19.0 %all_to_all.10 = bf16[16,4,8192]{2,1,0:T(4,128)(2,1)S(1)} all-to-all(bf16[16,4,8192]{2,1,0:T(4,128)(2,1)S(1)} %copy.9), channel_id=1, replica_groups=mesh['tm'=16,'col'=16] {'tm'}, dimensions={0} | all-to-all | bytes 2097152 | tf_op jit(solution)/shard_map/all_to_all | solution.py:87
  111.5 1.1 reshape.92
  112.6 0.0 reduce-scatter.4.cloned.1.call-start
  112.7 224.9 %all-gather.2.cloned.1.call-done = bf16[1024,8192]{1,0:T(8,128)(2,1)} async-done(((bf16[64,8192]{1,0:T(8,128)(2,1)}), bf16[1024,8192]{1,0:T(8,128)(2,1)}) %all-gather.2.cloned.1.call-update) | async-done | bytes 16777232 | tf_op jit(solution)/shard_map/all_gather | solution.py:91
  337.6 8.9 %convolution_bitcast_fusion = f32[1024,64]{1,0:T(8,128)} fusion(bf16[64,8192]{1,0:T(8,128)(2,1)S(1)} %copy-done, bf16[1024,8192]{1,0:T(8,128)(2,1)} %all-gather.2.cloned.1.call-done), kind=kOutput, calls=%fused_computation.27 | convolution fusion | flops 1073741824 | bytes 18087936
  346.5 60.8 %reduce-scatter.4.cloned.1.call-done = f32[64,64]{1,0:T(8,128)} async-done(((f32[1024,64]{1,0:T(8,128)}), f32[64,64]{1,0:T(8,128)}) %reduce-scatter.4.cloned.1.call-update) | async-done | bytes 16400
  407.4 0.8 copy.18
  408.2 0.6 broadcast_multiply_fusion
  (9 shorter events, 0.1 us)
Async XLA Ops:
  6.5 8.1 %copy-start.2 = (f32[131072]{0:T(1024)S(1)}, f32[131072]{0:T(1024)}, u32[]{:S(2)}) copy-start(f32[131072]{0:T(1024)} %param.3) | copy-start | bytes 1572868
  8.8 20.9 %all-to-all-start = ((bf16[16,4,8192]{2,1,0:T(4,128)(2,1)}), bf16[16,4,8192]{2,1,0:T(4,128)(2,1)S(1)}, u32[]{:S(2)}, u32[]{:S(2)}) async-start(bf16[16,4,8192]{2,1,0:T(4,128)(2,1)} %reshape.89), calls=%async_computation | async-start | bytes 2097152 | tf_op jit(solution)/shard_map/all_to_all | solution.py:85
  14.6 323.0 %all-gather.2.cloned.1.call-start = ((), (), s32[]{:S(2)}) async-start(), calls=%async_computation.3 | async-start | bytes 17825792 | tf_op jit(solution)/shard_map/all_gather | solution.py:91
  31.6 5.7 %copy-start.1 = (bf16[16,4,32,256]{3,2,1,0:T(8,128)(2,1)S(1)}, bf16[16,4,32,256]{3,2,1,0:T(8,128)(2,1)}, u32[]{:S(2)}) copy-start(bf16[16,4,32,256]{3,2,1,0:T(8,128)(2,1)} %reshape.107) | copy-start | bytes 3145732
  112.6 225.0 %copy-start = (bf16[64,8192]{1,0:T(8,128)(2,1)S(1)}, bf16[64,8192]{1,0:T(8,128)(2,1)}, u32[]{:S(2)}) copy-start(bf16[64,8192]{1,0:T(8,128)(2,1)} %reshape.92) | copy-start | bytes 3145732
  112.6 294.8 %reduce-scatter.4.cloned.1.call-start = ((), (), s32[]{:S(2)}) async-start(), calls=%async_computation.4 | async-start | bytes 557056
Sparse Core Ops, SparseCore 0:
  112.7 224.8 all-gather.1
  346.6 60.6 reduce-scatter.3
where the time goes:
time: 420 us; the launch traced here: 416 us
  waiting for transfers between devices  298 us (71%)
  matrix products  68.2 us (16%)
  blocking collectives  19 us (5%)
  between operations  13.8 us (3%)
  local copies, waits for them, and re-layouts  7.8 us (2%)
  starting transfers between devices  5.86 us (1%)
    all_gather x1, waiting for transfers between devices, on_device(): lax.all_gather(whitened, 'col', axis=0, tiled=True)  225 us
    unnamed x3, waiting for transfers between devices  60.9 us
    dot_general x10, matrix products, mixed(): return jnp.einsum(form, left, right, precision=lax.Precision.HIGHEST)  40.2 us
    all_to_all x1, blocking collectives, on_device(): lax.all_to_all(filtered, 'tm', split_axis=0, concat_axis=0, tiled=True)  19 us
    all_to_all x1, waiting for transfers between devices, on_device(): lax.all_to_all(grouped, 'tm', split_axis=0, concat_axis=0, tiled=True)  12.7 us
    dot_general x2, matrix products, exact_first(): jnp.einsum('kja,jban->kbn', upper, values, preferred_element_type=jnp.flo...  10.1 us
    dot_general x2, matrix products, exact_first(): jnp.einsum('kja,jban->kbn', lower, values, preferred_element_type=jnp.flo...  9.04 us
    unnamed x1, matrix products  8.9 us
  transfers between devices with their start and end apart: 3, of which 3 were waited for; matrix products, arithmetic and copies ran while one was open for 1% of the time, Pallas kernels for 0%

commit v1 on v0

v1 whole, which is shorter than its diff:
```python
import math

import jax
import jax.numpy as jnp
import numpy as np
from jax import lax
from jax.experimental import pallas as pl
from jax.experimental.pallas import tpu as pltpu
from jax.sharding import Mesh
from jax.sharding import PartitionSpec as P

EPOCHS = 131072
SLOW = 512
FAST = 256
HALF = SLOW // 2
KEPT = HALF + 8
COLUMNS = 4
DEVICES = 256

EVERY = ("z", "yh", "yl", "x", "core")
ROWS = ("z", "yh")
TIMES = ("yl", "x", "core")
CHIPS = ("yl", "x")

F32 = jnp.float32
BF16 = jnp.bfloat16


def split_table(table):
    upper = table.astype(np.float32).astype(BF16)
    lower = (table - upper.astype(np.float64)).astype(np.float32).astype(BF16)
    return upper, lower


def phase(rows, cols, length):
    index = np.outer(np.asarray(rows, np.int64), np.asarray(cols, np.int64)) % length
    return index * (2.0 * math.pi / length)


def host_tables():
    slow = np.arange(SLOW)
    cosine = np.cos(phase(np.arange(HALF + 1), slow, SLOW))
    sine = np.sin(phase(np.arange(1, HALF), slow, SLOW))
    real_fold = np.concatenate([cosine[:HALF], cosine[HALF:], -sine], axis=0)
    turn = phase(np.arange(KEPT), np.arange(FAST), EPOCHS)
    inner = phase(np.arange(FAST), np.arange(FAST), FAST)
    complex_inner = np.block(
        [[np.cos(inner), -np.sin(inner)], [np.sin(inner), np.cos(inner)]]
    )
    odd = 2 * np.arange(HALF) + 1
    spread = np.cos(phase(odd, odd, 8 * HALF)) * math.sqrt(2.0 / HALF)
    spread_upper, _ = split_table(spread)
    norm = math.sqrt(float((spread_upper.astype(np.float64)[0] ** 2).sum()))
    return (
        split_table(real_fold),
        (np.cos(turn).astype(np.float32), np.sin(turn).astype(np.float32)),
        split_table(complex_inner),
        spread_upper,
        norm,
    )


def dot(left, right):
    return jnp.dot(left, right, preferred_element_type=F32)


def deal_kernel(panel_ref, out_ref, spread_ref):
    runs = panel_ref.shape[1] // FAST
    stride = COLUMNS * runs
    for column in range(COLUMNS):
        for run in range(runs):
            for half in range(FAST // 128):
                lane = run * FAST + half * 128
                piece = panel_ref[column * 16 : (column + 1) * 16, lane : lane + 128]
                spread_ref[half, pl.ds(column * runs + run, 16, stride=stride), :] = piece.astype(F32)
    for half in range(FAST // 128):
        out_ref[:, half * 128 : (half + 1) * 128] = spread_ref[half].astype(BF16)


def deal(panel):
    rows, epochs = panel.shape
    runs = epochs // FAST
    return pl.pallas_call(
        deal_kernel,
        out_shape=jax.ShapeDtypeStruct((16 * COLUMNS * runs, FAST), BF16),
        scratch_shapes=[pltpu.VMEM((FAST // 128, 16 * COLUMNS * runs, 128), F32)],
        name="deal",
    )(panel)


def filter_kernel(
    series_ref,
    fold_hi,
    fold_lo,
    turn_cos,
    turn_sin,
    inner_hi,
    inner_lo,
    gain_ref,
    spread,
    out_ref,
    lines_ref,
):
    blocks = series_ref.shape[0]
    runs = SLOW // blocks
    first_row = lax.broadcasted_iota(jnp.int32, (HALF, FAST), 0) == 0
    gain = gain_ref[0:HALF, :]
    edge_gain = gain_ref[HALF : HALF + 1, :]
    tiles = 2 * FAST // 128
    for column in range(COLUMNS):
        series = jnp.concatenate(
            [series_ref[j, column * runs : (column + 1) * runs, :] for j in range(blocks)], axis=0
        )
        folded = dot(fold_hi[...], series) + dot(fold_lo[...], series)
        real = folded[0:HALF]
        imag = folded[HALF:SLOW]
        edge = imag[0:1]
        cosine = turn_cos[0:HALF, :]
        sine = turn_sin[0:HALF, :]
        turned_re = real * cosine + imag * sine
        turned_im = jnp.where(first_row, 0.0, imag * cosine - real * sine)
        edge_re = edge * turn_cos[HALF : HALF + 1, :]
        edge_im = -edge * turn_sin[HALF : HALF + 1, :]
        edge_row = jnp.concatenate([edge_re, edge_im], axis=1)
        turned = jnp.concatenate(
            [
                jnp.concatenate([turned_re, turned_im], axis=1),
                jnp.broadcast_to(edge_row, (16, 2 * FAST)),
            ],
            axis=0,
        )
        upper = turned.astype(BF16)
        lower = (turned - upper.astype(F32)).astype(BF16)
        lines = dot(upper, inner_hi[...]) + dot(upper, inner_lo[...]) + dot(lower, inner_hi[...])
        line_re = lines[0:HALF, 0:FAST] * gain
        line_im = lines[0:HALF, FAST:] * gain
        edge_line = (lines[HALF : HALF + 1, 0:FAST] + lines[HALF : HALF + 1, FAST:]) * edge_gain
        first = line_re + line_im
        line_re = jnp.where(first_row, first, line_re)
        line_im = jnp.where(first_row, jnp.broadcast_to(edge_line, (HALF, FAST)), line_im)
        packed = jnp.concatenate([line_re, line_im], axis=1)
        upper = packed.astype(BF16)
        lower = (packed - upper.astype(F32)).astype(BF16)
        mixed = dot(spread[...], upper) + dot(spread[...], lower)
        for tile in range(tiles):
            lines_ref[pl.ds(column * tiles + tile, HALF, stride=COLUMNS * tiles), :] = mixed[
                :, tile * 128 : (tile + 1) * 128
            ]
    out_ref[...] = lines_ref[...].astype(BF16)


def filter_columns(series, tables, gain):
    (fold_hi, fold_lo), (turn_cos, turn_sin), (inner_hi, inner_lo), spread, _ = tables
    rows = DEVICES * COLUMNS * 2 * FAST // 128
    return pl.pallas_call(
        filter_kernel,
        out_shape=jax.ShapeDtypeStruct((rows, 128), BF16),
        scratch_shapes=[pltpu.VMEM((rows, 128), F32)],
        name="filter",
    )(
        series,
        jnp.asarray(fold_hi),
        jnp.asarray(fold_lo),
        jnp.asarray(turn_cos),
        jnp.asarray(turn_sin),
        jnp.asarray(inner_hi),
        jnp.asarray(inner_lo),
        gain,
        jnp.asarray(spread),
    )


def gather_kernel(lines_ref, out_ref, wide_ref):
    tiles = 2 * FAST // 128
    wide_ref[...] = lines_ref[...].astype(F32)
    for column in range(COLUMNS):
        for tile in range(tiles):
            rows = wide_ref[
                pl.ds(column * tiles + tile, DEVICES, stride=COLUMNS * tiles), :
            ].astype(BF16)
            for b in range(16):
                out_ref[
                    b * 64 + column * 16 : b * 64 + column * 16 + 16, tile * 128 : (tile + 1) * 128
                ] = rows[b * 16 : b * 16 + 16, :]


def gather_rows(lines):
    return pl.pallas_call(
        gather_kernel,
        out_shape=jax.ShapeDtypeStruct((DEVICES * COLUMNS, 2 * FAST), BF16),
        scratch_shapes=[pltpu.VMEM(lines.shape, F32)],
        name="gather_rows",
    )(lines)


def gram_kernel(core_ref, mine_ref, other_ref, out_ref):
    core = core_ref[0]
    nt = (((1,), (1,)), ((), ()))
    for block in range(8):
        start = pl.multiple_of(128 * block + 64 * core, 64)
        own = lax.dot_general(
            mine_ref[pl.ds(start, 64), :], mine_ref[...], nt, preferred_element_type=F32
        )
        own += lax.dot_general(
            other_ref[pl.ds(start, 64), :], other_ref[...], nt, preferred_element_type=F32
        )
        out_ref[block * 64 : (block + 1) * 64, :] = own.astype(BF16)


def gram(core, mine, other):
    return pl.pallas_call(
        gram_kernel,
        out_shape=jax.ShapeDtypeStruct((512, mine.shape[0]), BF16),
        in_specs=[
            pl.BlockSpec(memory_space=pltpu.SMEM),
            pl.BlockSpec(memory_space=pltpu.VMEM),
            pl.BlockSpec(memory_space=pltpu.VMEM),
        ],
        name="gram",
    )(core, mine, other)


def fold_kernel(parts_ref, out_ref):
    total = parts_ref[0].astype(F32)
    for chip in range(1, parts_ref.shape[0]):
        total += parts_ref[chip].astype(F32)
    lane = lax.broadcasted_iota(jnp.int32, (32, 128), 1) < 64
    for pair in range(8):
        upper = total[0:32, pair * 128 : (pair + 1) * 128]
        lower = total[32:64, pair * 128 : (pair + 1) * 128]
        out_ref[2 * pair] = jnp.where(lane, upper, pltpu.roll(lower, 64, 1))
        out_ref[2 * pair + 1] = jnp.where(lane, pltpu.roll(upper, 64, 1), lower)


def fold(parts):
    return pl.pallas_call(
        fold_kernel,
        out_shape=jax.ShapeDtypeStruct((16, 32, 128), F32),
        name="fold",
    )(parts)


def finish_kernel(parts_ref, out_ref):
    total = parts_ref[0]
    for part in range(1, parts_ref.shape[0]):
        total += parts_ref[part]
    block = jnp.concatenate([total[:, 0:64], total[:, 64:128]], axis=0)
    out_ref[...] = block.T


def finish(parts):
    return pl.pallas_call(
        finish_kernel,
        out_shape=jax.ShapeDtypeStruct((64, 64), F32),
        name="finish",
    )(parts)


def gain_table(response, norm):
    grid = response.reshape(FAST, SLOW)
    mirror = jnp.concatenate(
        [
            jnp.roll(jnp.flip(grid[:, 0:1], axis=0), 1, axis=0),
            jnp.flip(grid[:, HALF : SLOW], axis=(0, 1)),
        ],
        axis=1,
    )
    even = (grid[:, : HALF + 1] + mirror) * 0.5
    weight = np.full((1, HALF + 1), math.sqrt(2.0))
    weight[0, 0] = weight[0, HALF] = 1.0
    even = even * jnp.asarray((weight / (EPOCHS * norm)).astype(np.float32))
    return jnp.pad(even.T, ((0, KEPT - HALF - 1), (0, 0)))


def exchange(values, axes):
    return lax.all_to_all(values, axes, split_axis=0, concat_axis=0, tiled=True)


def on_device(panel, response):
    tables = host_tables()
    gain = gain_table(response, tables[4])
    dealt = deal(panel).reshape(16, -1, FAST)
    series = exchange(dealt, TIMES)
    lines = filter_columns(series, tables, gain)
    lines = exchange(lines.reshape(DEVICES, -1, 128), EVERY).reshape(lines.shape)
    mine = gather_rows(lines)
    other = lax.ppermute(mine, "core", [(0, 1), (1, 0)])
    core = lax.axis_index("core").astype(jnp.int32).reshape(1)
    part = gram(core, mine, other)
    parts = exchange(part.reshape(8, 64, -1), CHIPS)
    folded = exchange(fold(parts), ROWS)
    return finish(folded)


def solution(mesh):
    fine = Mesh(mesh.devices.reshape(2, 4, 2, 8, 2), ("yl", "x", "core", "z", "yh"))
    return jax.shard_map(
        on_device,
        mesh=fine,
        in_specs=(P(ROWS, TIMES), P()),
        out_specs=P(ROWS, TIMES),
        check_vma=False,
    )
```

time: 420 us -> 138 us (0.33)
  waiting for transfers between devices: 298 us -> 13.4 us
  matrix products: 68.2 us -> 0 us
  blocking collectives: 19 us -> 82.2 us
  Pallas kernels: 0 us -> 29.7 us
  between operations: 13.8 us -> 0.07 us
    all_gather x1 -> x0, waiting for transfers between devices: 225 us -> none  [on_device(): lax.all_gather(whitened, 'col', axis=0, tiled=True)]
    all_to_all x1 -> x3, blocking collectives: 19 us -> 82.2 us  [exchange(): return lax.all_to_all(values, axes, split_axis=0, concat_axis=0, tiled=True)]
    unnamed x3 -> x0, waiting for transfers between devices: 60.9 us -> none
    dot_general x14 -> x0, matrix products: 59.3 us -> none  [the longest x10 40.2 us: mixed(): return jnp.einsum(form, left, right, precision=lax.Precision.HIGHEST)]
    pallas_call x0 -> x6, Pallas kernels: none -> 29.7 us  [the longest x1 10.6 us: filter_columns(): pl.pallas_call(filter_kernel, out_shape=jax.ShapeDtypeStruct((rows, 128),...]
    unnamed x1 -> x0, matrix products: 8.9 us -> none
    reshape x4 -> x1, local copies, waits for them, and re-layouts: 5.42 us -> 0.08 us  [gain_table(): grid = response.reshape(FAST, SLOW)]
  transfers between devices with their start and end apart: 3 -> 2, of which waited for: 3 -> 2; matrix products, arithmetic and copies ran while one was open for 1% -> 2% of each run, Pallas kernels for 0% -> 0%
where the time goes in v1:
time: 138 us
  blocking collectives  82.2 us (60%)
  Pallas kernels  29.7 us (22%)
  waiting for transfers between devices  13.4 us (10%)
  starting transfers between devices  5.91 us (4%)
  local copies, waits for them, and re-layouts  5.75 us (4%)
    all_to_all x3, blocking collectives, exchange(): return lax.all_to_all(values, axes, split_axis=0, concat_axis=0, tiled=True)  82.2 us
    pallas_call x1, Pallas kernels, filter_columns(): pl.pallas_call(filter_kernel, out_shape=jax.ShapeDtypeStruct((rows, 128),...  10.6 us
    all_to_all x1, waiting for transfers between devices, exchange(): return lax.all_to_all(values, axes, split_axis=0, concat_axis=0, tiled=True)  10.5 us
    pallas_call x1, Pallas kernels, gram(): pl.pallas_call(gram_kernel, out_shape=jax.ShapeDtypeStruct((512, mine.sha...  7.69 us
    all_to_all x1, starting transfers between devices, exchange(): return lax.all_to_all(values, axes, split_axis=0, concat_axis=0, tiled=True)  5.91 us
    pallas_call x1, Pallas kernels, deal(): pl.pallas_call(deal_kernel, out_shape=jax.ShapeDtypeStruct((16 * COLUMNS...  4.28 us
    pallas_call x1, Pallas kernels, gather_rows(): pl.pallas_call(gather_kernel, out_shape=jax.ShapeDtypeStruct((DEVICES * C...  3.21 us
    unnamed x15, local copies, waits for them, and re-layouts  3.15 us
  transfers between devices with their start and end apart: 2, of which 2 were waited for; matrix products, arithmetic and copies ran while one was open for 2% of the time, Pallas kernels for 0%

profile of v1, /device:TPU:8, one launch (start us, length us, event | category | flops | bytes accessed | tf_op | source)
XLA Modules:
  0.0 137.8 jit_solution(440485105914418865)
XLA Ops:
  0.0 4.3 %deal.1 = bf16[2048,256]{1,0:T(8,128)(2,1)} custom-call(bf16[64,8192]{1,0:T(8,128)(2,1)} %panel_ref.1), custom_call_target="tpu_custom_call" | custom-call | tf_op jit(solution)/shard_map/deal/pallas_call | solution.py:83
  4.3 0.0 copy-start.3
  4.3 5.9 %all-to-all-start = ((bf16[16,128,256]{2,1,0:T(8,128)(2,1)}), bf16[16,128,256]{2,1,0:T(8,128)(2,1)S(1)}, u32[]{:S(2)}, u32[]{:S(2)}) async-start(bf16[16,128,256]{2,1,0:T(8,128)(2,1)} %bitcast.10), calls=%async_computation | async-start | bytes 2097152 | tf_op jit(solution)/shard_map/all_to_all | solution.py:276
  10.2 0.0 copy-done.3
  10.2 0.1 reshape.22
  10.3 0.0 copy-start.1
  10.3 0.6 slice.27
  10.9 0.2 copy-done.1
  11.1 0.1 copy.17
  11.2 0.2 reverse.2
  11.4 0.1 slice.30
  11.5 0.1 copy.15
  11.6 0.8 slice-done
  12.4 0.1 copy.18
  12.6 0.0 copy-start.4
  12.6 0.4 rev.6
  13.0 0.3 copy-done.4
  13.3 0.7 fusion.1
  14.0 0.7 pad.4.gain_ref
  14.7 10.5 %all-to-all-done.series_ref = bf16[16,128,256]{2,1,0:T(8,128)(2,1)S(1)} async-done(((bf16[16,128,256]{2,1,0:T(8,128)(2,1)}), bf16[16,128,256]{2,1,0:T(8,128)(2,1)S(1)}, u32[]{:S(2)}, u32[]{:S(2)}) %all-to-all-start) | async-done | bytes 1048608 | tf_op jit(solution)/shard_map/all_to_all | solution.py:276
  25.3 1.0 copy-done
  26.3 10.6 %filter.1 = bf16[4096,128]{1,0:T(8,128)(2,1)} custom-call(bf16[16,128,256]{2,1,0:T(8,128)(2,1)} %copy-done, bf16[512,512]{1,0:T(8,128)(2,1)} %constant.28.clone.fold_hi, bf16[512,512]{1,0:T(8,128)(2,1)} %constant.29.clone.fold_lo, f32[264,256]{1,0:T(8,128)} %constant.30.clone.turn_cos, f32[264,256]{1,0:T(8,128)} %constant.31.clone.turn_sin, ...), custom_call_target="tpu_custom_call" | custom-call | tf_op jit(solution)/shard_map/filter/pallas_call | solution.py:155
  36.9 44.3 %all_to_all.20 = bf16[256,16,128]{2,1,0:T(8,128)(2,1)} all-to-all(bf16[256,16,128]{2,1,0:T(8,128)(2,1)} %bitcast.9), channel_id=1, replica_groups=mesh['yl'=2,'x'=4,'core'=2,'z'=8,'yh'=2] {'z','yh','yl','x','core'}, dimensions={0} | all-to-all | bytes 2097152 | tf_op jit(solution)/shard_map/all_to_all | solution.py:276
  81.2 3.2 %gather_rows.1.mine_ref = bf16[1024,512]{1,0:T(8,128)(2,1)} custom-call(bf16[4096,128]{1,0:T(8,128)(2,1)} %bitcast.12), custom_call_target="tpu_custom_call" | custom-call | tf_op jit(solution)/shard_map/gather_rows/pallas_call | solution.py:188
  84.4 0.0 collective-permute-start
  84.4 2.9 %collective-permute-done.other_ref = bf16[1024,512]{1,0:T(8,128)(2,1)S(1)} collective-permute-done((bf16[1024,512]{1,0:T(8,128)(2,1)}, bf16[1024,512]{1,0:T(8,128)(2,1)S(1)}, u32[]{:S(2)}, u32[]{:S(2)}) %collective-permute-start) | collective-permute-done | bytes 1048608 | tf_op jit(solution)/shard_map/ppermute | solution.py:287
  87.3 1.0 copy-done.2
  88.2 7.7 %gram.1 = bf16[512,1024]{1,0:T(8,128)(2,1)} custom-call(s32[1]{0:T(128)} %bitcast.core_ref, bf16[1024,512]{1,0:T(8,128)(2,1)} %gather_rows.1.mine_ref, bf16[1024,512]{1,0:T(8,128)(2,1)} %copy-done.2), custom_call_target="tpu_custom_call" | custom-call | tf_op jit(solution)/shard_map/gram/pallas_call | solution.py:211
  95.9 19.6 %all_to_all.21.parts_ref = bf16[8,64,1024]{2,1,0:T(8,128)(2,1)} all-to-all(bf16[8,64,1024]{2,1,0:T(8,128)(2,1)} %bitcast.11), channel_id=1, replica_groups=mesh['yl'=2,'x'=4,'core'=2,'z'=8,'yh'=2] {'yl','x'}, dimensions={0} | all-to-all | bytes 2097152 | tf_op jit(solution)/shard_map/all_to_all | solution.py:276
  115.6 2.2 %fold.1 = f32[16,32,128]{2,1,0:T(8,128)} custom-call(bf16[8,64,1024]{2,1,0:T(8,128)(2,1)} %all_to_all.21.parts_ref), custom_call_target="tpu_custom_call" | custom-call | tf_op jit(solution)/shard_map/fold/pallas_call | solution.py:236
  117.7 18.3 %all_to_all.22.parts_ref = f32[16,32,128]{2,1,0:T(8,128)} all-to-all(f32[16,32,128]{2,1,0:T(8,128)} %fold.1), channel_id=1, replica_groups=mesh['yl'=2,'x'=4,'core'=2,'z'=8,'yh'=2] {'z','yh'}, dimensions={0} | all-to-all | bytes 524288 | tf_op jit(solution)/shard_map/all_to_all | solution.py:276
  136.1 1.7 %finish.1 = f32[64,64]{1,0:T(8,128)} custom-call(f32[16,32,128]{2,1,0:T(8,128)} %all_to_all.22.parts_ref), custom_call_target="tpu_custom_call" | custom-call | tf_op jit(solution)/shard_map/finish/pallas_call | solution.py:252
  (5 shorter events, 0.1 us)
Async XLA Ops:
  4.3 5.9 %copy-start.3 = (f32[131072]{0:T(1024)S(1)}, f32[131072]{0:T(1024)}, u32[]{:S(2)}) copy-start(f32[131072]{0:T(1024)} %param.11) | copy-start | bytes 1572868
  4.3 21.0 %all-to-all-start = ((bf16[16,128,256]{2,1,0:T(8,128)(2,1)}), bf16[16,128,256]{2,1,0:T(8,128)(2,1)S(1)}, u32[]{:S(2)}, u32[]{:S(2)}) async-start(bf16[16,128,256]{2,1,0:T(8,128)(2,1)} %bitcast.10), calls=%async_computation | async-start | bytes 2097152 | tf_op jit(solution)/shard_map/all_to_all | solution.py:276
  10.3 0.8 copy-start.1
  11.5 1.0 slice-start
  12.6 0.7 copy-start.4
  25.3 1.0 copy-start
  84.4 2.9 %collective-permute-start = (bf16[1024,512]{1,0:T(8,128)(2,1)}, bf16[1024,512]{1,0:T(8,128)(2,1)S(1)}, u32[]{:S(2)}, u32[]{:S(2)}) collective-permute-start(bf16[1024,512]{1,0:T(8,128)(2,1)} %gather_rows.1.mine_ref), channel_id=1, source_target_pairs={{0,16},{16,0},{1,17},{17,1},{2,18},{18,2},{3,19},{19,3},{4,20},{20... | collective-permute-start | bytes 3145736 | tf_op jit(solution)/shard_map/ppermute | solution.py:287
  87.3 1.0 copy-start.2

commit v2 on v1

v2 whole, which is shorter than its diff:
```python
import math

import jax
import jax.numpy as jnp
import numpy as np
from jax import lax
from jax.experimental import pallas as pl
from jax.experimental.pallas import tpu as pltpu
from jax.sharding import Mesh
from jax.sharding import PartitionSpec as P

EPOCHS = 131072
SLOW = 512
FAST = 256
HALF = SLOW // 2
KEPT = HALF + 8
CHUNKS = 1
DEVICES = 256
MIB = 1 << 20
FILTER_VMEM = 24 * MIB
GRAM_VMEM = 24 * MIB
FOLD_VMEM = 16 * MIB

EVERY = ("z", "yh", "yl", "x", "core")
ROWS = ("z", "yh")
TIMES = ("yl", "x", "core")
CHIPS = ("yl", "x")

F32 = jnp.float32
BF16 = jnp.bfloat16


def split_table(table):
    upper = table.astype(np.float32).astype(BF16)
    lower = (table - upper.astype(np.float64)).astype(np.float32).astype(BF16)
    return upper, lower


def phase(rows, cols, length):
    index = np.outer(np.asarray(rows, np.int64), np.asarray(cols, np.int64)) % length
    return index * (2.0 * math.pi / length)


def host_tables():
    slow = np.arange(SLOW)
    cosine = np.cos(phase(np.arange(HALF + 1), slow, SLOW))
    sine = np.sin(phase(np.arange(1, HALF), slow, SLOW))
    real_fold = np.concatenate([cosine[:HALF], cosine[HALF:], -sine], axis=0)
    turn = phase(np.arange(KEPT), np.arange(FAST), EPOCHS)
    inner = phase(np.arange(FAST), np.arange(FAST), FAST)
    complex_inner = np.block(
        [[np.cos(inner), -np.sin(inner)], [np.sin(inner), np.cos(inner)]]
    )
    odd = 2 * np.arange(HALF) + 1
    spread = np.cos(phase(odd, odd, 8 * HALF)) * math.sqrt(2.0 / HALF)
    spread_upper, _ = split_table(spread)
    norm = math.sqrt(float((spread_upper.astype(np.float64)[0] ** 2).sum()))
    return (
        split_table(real_fold),
        (np.cos(turn).astype(np.float32), np.sin(turn).astype(np.float32)),
        split_table(complex_inner),
        spread_upper,
        norm,
    )


def dot(left, right):
    return jnp.dot(left, right, preferred_element_type=F32)


def join(parts, axis):
    return jnp.concatenate(parts, axis=axis)


def filter_kernel(
    series_ref,
    fold_hi,
    fold_lo,
    turn_cos,
    turn_sin,
    inner_hi,
    inner_lo,
    gain_ref,
    spread,
    out_ref,
    lines_ref,
):
    blocks, columns, runs, _ = series_ref.shape
    first_row = lax.broadcasted_iota(jnp.int32, (HALF, FAST), 0) == 0
    gain = gain_ref[0:HALF, :]
    edge_gain = gain_ref[HALF : HALF + 1, :]
    tiles = 2 * FAST // 128
    for column in range(columns):
        series = join([series_ref[j, column] for j in range(blocks)], 0)
        folded = dot(join([fold_hi[...], fold_lo[...]], 1), join([series, series], 0))
        real = folded[0:HALF]
        imag = folded[HALF:SLOW]
        edge = imag[0:1]
        cosine = turn_cos[0:HALF, :]
        sine = turn_sin[0:HALF, :]
        turned_re = real * cosine + imag * sine
        turned_im = jnp.where(first_row, 0.0, imag * cosine - real * sine)
        edge_re = edge * turn_cos[HALF : HALF + 1, :]
        edge_im = -edge * turn_sin[HALF : HALF + 1, :]
        edge_row = jnp.broadcast_to(join([edge_re, edge_im], 1), (16, 2 * FAST))
        turned = join([join([turned_re, turned_im], 1), edge_row], 0)
        upper = turned.astype(BF16)
        lower = (turned - upper.astype(F32)).astype(BF16)
        lines = dot(
            join([upper, upper, lower], 1), join([inner_hi[...], inner_lo[...], inner_hi[...]], 0)
        )
        line_re = lines[0:HALF, 0:FAST] * gain
        line_im = lines[0:HALF, FAST:] * gain
        edge_line = (lines[HALF : HALF + 1, 0:FAST] + lines[HALF : HALF + 1, FAST:]) * edge_gain
        first = line_re + line_im
        line_re = jnp.where(first_row, first, line_re)
        line_im = jnp.where(first_row, jnp.broadcast_to(edge_line, (HALF, FAST)), line_im)
        packed = join([line_re, line_im], 1)
        upper = packed.astype(BF16)
        lower = (packed - upper.astype(F32)).astype(BF16)
        mixed = dot(join([spread[...], spread[...]], 1), join([upper, lower], 0))
        for tile in range(tiles):
            lines_ref[pl.ds(tile * columns + column, HALF, stride=columns * tiles), :] = mixed[
                :, tile * 128 : (tile + 1) * 128
            ]
    out_ref[...] = lines_ref[...].astype(BF16)


def filter_columns(series, tables, gain):
    rows = DEVICES * series.shape[1] * 2 * FAST // 128
    return pl.pallas_call(
        filter_kernel,
        out_shape=jax.ShapeDtypeStruct((rows, 128), BF16),
        scratch_shapes=[pltpu.VMEM((rows, 128), F32)],
        compiler_params=pltpu.CompilerParams(vmem_limit_bytes=FILTER_VMEM),
        cost_estimate=pl.CostEstimate(
            flops=2_000_000_000 * series.shape[1], bytes_accessed=4 * MIB, transcendentals=0
        ),
        name="filter",
    )(series, *tables[:6], gain, tables[6])


def gram_rows(core_ref, ref):
    start = 64 * core_ref[0]
    blocks = [ref[pl.ds(pl.multiple_of(128 * b + start, 64), 64), :] for b in range(8)]
    return join(blocks, 0)


def half_gram(core_ref, ref):
    return lax.dot_general(
        gram_rows(core_ref, ref), ref[...], (((1,), (1,)), ((), ())), preferred_element_type=F32
    )


def gram_mine_kernel(core_ref, mine_ref, out_ref):
    out_ref[...] = half_gram(core_ref, mine_ref)


def gram_other_kernel(core_ref, other_ref, begun_ref, out_ref):
    out_ref[...] = (begun_ref[...] + half_gram(core_ref, other_ref)).astype(BF16)


def gram(kernel, dtype, name, core, *arrays):
    return pl.pallas_call(
        kernel,
        out_shape=jax.ShapeDtypeStruct((512, 1024), dtype),
        in_specs=[pl.BlockSpec(memory_space=pltpu.SMEM)]
        + [pl.BlockSpec(memory_space=pltpu.VMEM)] * len(arrays),
        compiler_params=pltpu.CompilerParams(vmem_limit_bytes=GRAM_VMEM),
        cost_estimate=pl.CostEstimate(
            flops=1_000_000_000, bytes_accessed=4 * MIB, transcendentals=0
        ),
        name=name,
    )(core, *arrays)


def fold_kernel(parts_ref, out_ref):
    total = parts_ref[0].astype(F32)
    for chip in range(1, parts_ref.shape[0]):
        total += parts_ref[chip].astype(F32)
    width = 64 // CHUNKS
    group = lax.broadcasted_iota(jnp.int32, (32, 128), 1) // width
    for b in range(16):
        packed = None
        for half in range(2):
            for chunk in range(CHUNKS):
                lane = chunk * (1024 // CHUNKS) + b * width
                tile = lane // 128 * 128
                piece = total[32 * half : 32 * half + 32, tile : tile + 128]
                target = 64 * half + width * chunk
                shift = (target - (lane - tile)) % 128
                piece = pltpu.roll(piece, shift, 1) if shift else piece
                slot = group == target // width
                packed = piece if packed is None else jnp.where(slot, piece, packed)
        out_ref[b] = packed


def fold(parts):
    return pl.pallas_call(
        fold_kernel,
        out_shape=jax.ShapeDtypeStruct((16, 32, 128), F32),
        compiler_params=pltpu.CompilerParams(vmem_limit_bytes=FOLD_VMEM),
        name="fold",
    )(parts)


def finish_kernel(parts_ref, out_ref):
    total = parts_ref[0]
    for part in range(1, parts_ref.shape[0]):
        total += parts_ref[part]
    block = join([total[:, 0:64], total[:, 64:128]], 0)
    out_ref[...] = block.T


def finish(parts):
    return pl.pallas_call(
        finish_kernel,
        out_shape=jax.ShapeDtypeStruct((64, 64), F32),
        compiler_params=pltpu.CompilerParams(vmem_limit_bytes=FOLD_VMEM),
        name="finish",
    )(parts)


def gain_table(response, norm):
    grid = response.reshape(FAST, SLOW)
    mirror = jnp.concatenate(
        [
            jnp.roll(jnp.flip(grid[:, 0:1], axis=0), 1, axis=0),
            jnp.flip(grid[:, HALF : SLOW], axis=(0, 1)),
        ],
        axis=1,
    )
    even = (grid[:, : HALF + 1] + mirror) * 0.5
    weight = np.full((1, HALF + 1), math.sqrt(2.0))
    weight[0, 0] = weight[0, HALF] = 1.0
    even = even * jnp.asarray((weight / (EPOCHS * norm)).astype(np.float32))
    return jnp.pad(even.T, ((0, KEPT - HALF - 1), (0, 0)))


def exchange(values, axes):
    return lax.all_to_all(values, axes, split_axis=0, concat_axis=0, tiled=True)


def on_device(panel, response):
    (fold_hi, fold_lo), (turn_cos, turn_sin), (inner_hi, inner_lo), spread, norm = host_tables()
    tables = [
        jnp.asarray(table)
        for table in (fold_hi, fold_lo, turn_cos, turn_sin, inner_hi, inner_lo, spread)
    ]
    gain = gain_table(response, norm)
    tiles = 2 * FAST // 128
    rows = panel.shape[0] // CHUNKS
    columns = rows // 16
    series = []
    for chunk in range(CHUNKS):
        part = panel[chunk * rows : (chunk + 1) * rows].reshape(16, columns, -1, FAST)
        series.append(exchange(part, TIMES))
    lines = []
    for part in series:
        part = filter_columns(part, tables, gain)
        lines.append(exchange(part.reshape(DEVICES, tiles * columns, 128), EVERY))
    mine = lines[0].reshape(DEVICES, tiles, columns, 128).transpose(0, 2, 1, 3)
    mine = mine.reshape(DEVICES * columns, 2 * FAST)
    other = lax.ppermute(mine, "core", [(0, 1), (1, 0)])
    core = lax.axis_index("core").astype(jnp.int32).reshape(1)
    begun = gram(gram_mine_kernel, F32, "gram_mine", core, mine)
    part = gram(gram_other_kernel, BF16, "gram_other", core, other, begun)
    parts = exchange(part.reshape(8, 64, -1), CHIPS)
    folded = exchange(fold(parts), ROWS)
    return finish(folded)


def solution(mesh):
    fine = Mesh(mesh.devices.reshape(2, 4, 2, 8, 2), ("yl", "x", "core", "z", "yh"))
    return jax.shard_map(
        on_device,
        mesh=fine,
        in_specs=(P(ROWS, TIMES), P()),
        out_specs=P(ROWS, TIMES),
        check_vma=False,
    )
```

time: 138 us -> 119 us (0.86)
  Pallas kernels: 29.7 us -> 10 us
  local copies, waits for them, and re-layouts: 5.75 us -> 15.7 us
  waiting for transfers between devices: 13.4 us -> 5.24 us
  blocking collectives: 82.2 us -> 79.1 us
    pallas_call x3 -> x2, Pallas kernels: 15.2 us -> 1.47 us  [gram(): pl.pallas_call(kernel, out_shape=jax.ShapeDtypeStruct((512, 1024), dtype)...]
    all_to_all x1, waiting for transfers between devices: 10.5 us -> 3.34 us  [exchange(): return lax.all_to_all(values, axes, split_axis=0, concat_axis=0, tiled=True)]
    unnamed x15 -> x27, local copies, waits for them, and re-layouts: 3.15 us -> 8.15 us
    all_to_all x3, blocking collectives: 82.2 us -> 79.1 us  [exchange(): return lax.all_to_all(values, axes, split_axis=0, concat_axis=0, tiled=True)]
    pallas_call x1, Pallas kernels: 10.6 us -> 7.51 us  [filter_columns(): pl.pallas_call(filter_kernel, out_shape=jax.ShapeDtypeStruct((rows, 128),...]
    rev x1, local copies, waits for them, and re-layouts: 0.37 us -> 3.12 us  [gain_table(): jnp.flip(grid[:, HALF:SLOW], axis=(0, 1))]
    pallas_call x1, Pallas kernels: 2.17 us -> 0.24 us  [fold(): pl.pallas_call(fold_kernel, out_shape=jax.ShapeDtypeStruct((16, 32, 128),...]
    slice x1, local copies, waits for them, and re-layouts: 0.03 us -> 1.91 us  [gain_table(): even = (grid[:, :HALF + 1] + mirror) * 0.5]
  transfers between devices with their start and end apart: 2 -> 2, of which waited for: 2 -> 2; matrix products, arithmetic and copies ran while one was open for 2% -> 10% of each run, Pallas kernels for 0% -> 1%
where the time goes in v2:
time: 119 us; the launch traced here: 118 us
  blocking collectives  79.1 us (66%)
  local copies, waits for them, and re-layouts  15.7 us (13%)
  Pallas kernels  10 us (8%)
  starting transfers between devices  5.87 us (5%)
  waiting for transfers between devices  5.24 us (4%)
  other arithmetic  1.7 us (1%)
    all_to_all x3, blocking collectives, exchange(): return lax.all_to_all(values, axes, split_axis=0, concat_axis=0, tiled=True)  79.1 us
    unnamed x27, local copies, waits for them, and re-layouts  8.15 us
    pallas_call x1, Pallas kernels, filter_columns(): pl.pallas_call(filter_kernel, out_shape=jax.ShapeDtypeStruct((rows, 128),...  7.51 us
    all_to_all x1, starting transfers between devices, exchange(): return lax.all_to_all(values, axes, split_axis=0, concat_axis=0, tiled=True)  5.78 us
    all_to_all x1, waiting for transfers between devices, exchange(): return lax.all_to_all(values, axes, split_axis=0, concat_axis=0, tiled=True)  3.34 us
    rev x1, local copies, waits for them, and re-layouts, gain_table(): jnp.flip(grid[:, HALF:SLOW], axis=(0, 1))  3.12 us
  transfers between devices with their start and end apart: 2, of which 2 were waited for; matrix products, arithmetic and copies ran while one was open for 10% of the time, Pallas kernels for 1%

profile of v2, /device:TPU:8, one launch (start us, length us, event | category | flops | bytes accessed | tf_op | source)
XLA Modules:
  0.0 117.7 jit_solution(5380071589655953893)
XLA Ops:
  0.0 2.5 %copy.27 = bf16[8,8,32,256]{3,2,1,0:T(8,128)(2,1)} copy(bf16[8,8,32,256]{3,1,2,0:T(8,128)(2,1)} %bitcast.24) | data formatting | bytes 2097152
  2.5 5.8 %all-to-all-start = ((bf16[16,4,32,256]{3,2,1,0:T(8,128)(2,1)}), bf16[16,4,32,256]{3,2,1,0:T(8,128)(2,1)S(1)}, u32[]{:S(2)}, u32[]{:S(2)}) async-start(bf16[16,4,32,256]{3,2,1,0:T(8,128)(2,1)} %bitcast.10), calls=%async_computation | async-start | bytes 2097152 | tf_op jit(solution)/shard_map/all_to_all | solution.py:241
  8.3 0.0 copy-start.9
  8.3 0.1 reshape.25
  8.4 0.6 slice.27
  9.0 0.2 copy-done.7
  9.2 0.7 slice.29
  10.0 0.0 copy-start.6
  10.0 1.9 %slice.26 = f32[256,257]{1,0:T(8,128)} slice(f32[256,512]{1,0:T(8,128)} %copy-done.7), slice={[0:256], [0:257]} | slice | bytes 526336 | tf_op jit(solution)/shard_map/slice | solution.py:233
  11.9 0.1 copy.25
  12.0 0.2 reverse.2
  12.2 0.1 slice.30
  12.2 1.1 copy.23
  13.4 1.8 %copy.26 = f32[256,256]{0,1:T(8,128)} copy(f32[256,256]{1,0:T(8,128)} %slice.29) | data formatting | bytes 524288
  15.2 3.1 %rev.6 = f32[256,256]{0,1:T(8,128)} reverse(f32[256,256]{0,1:T(8,128)} %copy.26), dimensions={0,1} | reverse | bytes 524288 | tf_op jit(solution)/shard_map/jit(_flip)/rev | solution.py:229
  18.3 1.7 %fusion.1 = f32[257,256]{1,0:T(8,128)S(1)} fusion(f32[256,257]{0,1:T(8,128)S(1)} %copy.23, f32[256,256]{0,1:T(8,128)} %rev.6, f32[255,1]{0,1:T(1,128)S(1)} %slice.30, f32[1,1]{0,1:T(1,128)} %bitcast.7, f32[257]{0:T(512)S(1)} %copy-done.9), kind=kLoop, calls=%fused_computation.3 | loop fusion | flops 263168 | bytes 790532 | tf_op jit(solution)/shard_map/transpose | solution.py:237
  20.0 3.3 %all-to-all-done.series_ref = bf16[16,4,32,256]{3,2,1,0:T(8,128)(2,1)S(1)} async-done(((bf16[16,4,32,256]{3,2,1,0:T(8,128)(2,1)}), bf16[16,4,32,256]{3,2,1,0:T(8,128)(2,1)S(1)}, u32[]{:S(2)}, u32[]{:S(2)}) %all-to-all-start) | async-done | bytes 1048608 | tf_op jit(solution)/shard_map/all_to_all | solution.py:241
  23.4 0.9 copy-done.4
  24.4 1.0 copy-done.5
  25.3 7.5 %filter.1 = bf16[4096,128]{1,0:T(8,128)(2,1)S(1)} custom-call(bf16[16,4,32,256]{3,2,1,0:T(8,128)(2,1)S(1)} %all-to-all-done.series_ref, bf16[512,512]{1,0:T(8,128)(2,1)S(1)} %copy-done.3, bf16[512,512]{1,0:T(8,128)(2,1)S(1)} %copy-done.2, f32[264,256]{1,0:T(8,128)S(1)} %copy-done.5, f32[264,256]{1,0:T(8,128)S(1)} %copy-done.4, ...), custom_call_target="tpu_custom_call" | custom-call | flops 8000000000 | bytes 4194304 | tf_op jit(solution)/shard_map/filter/pallas_call | solution.py:131
  32.8 44.0 %all_to_all.20 = bf16[256,16,128]{2,1,0:T(8,128)(2,1)S(1)} all-to-all(bf16[256,16,128]{2,1,0:T(8,128)(2,1)S(1)} %bitcast.21), channel_id=1, replica_groups=mesh['yl'=2,'x'=4,'core'=2,'z'=8,'yh'=2] {'z','yh','yl','x','core'}, dimensions={0} | all-to-all | bytes 2097152 | tf_op jit(solution)/shard_map/all_to_all | solution.py:241
  76.8 0.3 copy.21
  77.1 0.8 copy.22
  77.9 0.2 copy.30
  78.1 0.1 collective-permute-start
  78.2 0.7 gram_mine.1.begun_ref
  78.9 1.9 %collective-permute-done.other_ref = bf16[1024,512]{1,0:T(8,128)(2,1)S(1)} collective-permute-done((bf16[1024,512]{1,0:T(8,128)(2,1)S(1)}, bf16[1024,512]{1,0:T(8,128)(2,1)S(1)}, u32[]{:S(2)}, u32[]{:S(2)}) %collective-permute-start) | collective-permute-done | bytes 1048608 | tf_op jit(solution)/shard_map/ppermute | solution.py:264
  80.8 0.7 gram_other.1
  81.6 18.9 %all_to_all.21.parts_ref = bf16[8,64,1024]{2,1,0:T(8,128)(2,1)S(1)} all-to-all(bf16[8,64,1024]{2,1,0:T(8,128)(2,1)S(1)} %bitcast.18), channel_id=1, replica_groups=mesh['yl'=2,'x'=4,'core'=2,'z'=8,'yh'=2] {'yl','x'}, dimensions={0} | all-to-all | bytes 2097152 | tf_op jit(solution)/shard_map/all_to_all | solution.py:241
  100.4 0.2 fold.1
  100.7 16.3 %all_to_all.22.parts_ref = f32[16,32,128]{2,1,0:T(8,128)S(1)} all-to-all(f32[16,32,128]{2,1,0:T(8,128)S(1)} %fold.1), channel_id=1, replica_groups=mesh['yl'=2,'x'=4,'core'=2,'z'=8,'yh'=2] {'z','yh'}, dimensions={0} | all-to-all | bytes 524288 | tf_op jit(solution)/shard_map/all_to_all | solution.py:241
  116.9 0.8 finish.1
  (17 shorter events, 0.1 us)
Async XLA Ops:
  0.0 8.3 %copy-start.8 = (f32[131072]{0:T(1024)S(1)}, f32[131072]{0:T(1024)}, u32[]{:S(2)}) copy-start(f32[131072]{0:T(1024)} %param.11) | copy-start | bytes 1572868
  2.5 20.9 %all-to-all-start = ((bf16[16,4,32,256]{3,2,1,0:T(8,128)(2,1)}), bf16[16,4,32,256]{3,2,1,0:T(8,128)(2,1)S(1)}, u32[]{:S(2)}, u32[]{:S(2)}) async-start(bf16[16,4,32,256]{3,2,1,0:T(8,128)(2,1)} %bitcast.10), calls=%async_computation | async-start | bytes 2097152 | tf_op jit(solution)/shard_map/all_to_all | solution.py:241
  8.3 10.0 %copy-start.9 = (f32[257]{0:T(512)S(1)}, f32[257]{0:T(512)}, u32[]{:S(2)}) copy-start(f32[257]{0:T(512)} %constant.38) | copy-start | bytes 3088
  8.4 0.8 copy-start.7
  10.0 13.4 %copy-start = (bf16[512,512]{1,0:T(8,128)(2,1)S(1)}, bf16[512,512]{1,0:T(8,128)(2,1)}, u32[]{:S(2)}) copy-start(bf16[512,512]{1,0:T(8,128)(2,1)} %constant.32.clone.inner_lo) | copy-start | bytes 1572868
  10.0 13.4 %copy-start.1 = (bf16[512,512]{1,0:T(8,128)(2,1)S(1)}, bf16[512,512]{1,0:T(8,128)(2,1)}, u32[]{:S(2)}) copy-start(bf16[512,512]{1,0:T(8,128)(2,1)} %constant.31.clone.inner_hi) | copy-start | bytes 1572868
  10.0 13.4 %copy-start.2 = (bf16[512,512]{1,0:T(8,128)(2,1)S(1)}, bf16[512,512]{1,0:T(8,128)(2,1)}, u32[]{:S(2)}) copy-start(bf16[512,512]{1,0:T(8,128)(2,1)} %constant.28.clone.fold_lo) | copy-start | bytes 1572868
  10.0 13.4 %copy-start.3 = (bf16[512,512]{1,0:T(8,128)(2,1)S(1)}, bf16[512,512]{1,0:T(8,128)(2,1)}, u32[]{:S(2)}) copy-start(bf16[512,512]{1,0:T(8,128)(2,1)} %constant.27.clone.fold_hi) | copy-start | bytes 1572868
  10.0 13.4 %copy-start.6 = (bf16[256,256]{1,0:T(8,128)(2,1)S(1)}, bf16[256,256]{1,0:T(8,128)(2,1)}, u32[]{:S(2)}) copy-start(bf16[256,256]{1,0:T(8,128)(2,1)} %constant.33.clone.spread) | copy-start | bytes 393220
  23.4 1.0 copy-start.4
  24.4 1.0 copy-start.5
  78.1 2.7 %collective-permute-start = (bf16[1024,512]{1,0:T(8,128)(2,1)S(1)}, bf16[1024,512]{1,0:T(8,128)(2,1)S(1)}, u32[]{:S(2)}, u32[]{:S(2)}) collective-permute-start(bf16[1024,512]{1,0:T(8,128)(2,1)S(1)} %bitcast.19), channel_id=1, source_target_pairs={{0,16},{16,0},{1,17},{17,1},{2,18},{18,2},{3,19},{19,3},{4,20},{20... | collective-permute-start | bytes 3145736 | tf_op jit(solution)/shard_map/ppermute | solution.py:264

commit v3 on v2

v3 whole, which is shorter than its diff:
```python
import math

import jax
import jax.numpy as jnp
import numpy as np
from jax import lax
from jax.experimental import pallas as pl
from jax.experimental.pallas import tpu as pltpu
from jax.sharding import Mesh
from jax.sharding import PartitionSpec as P

EPOCHS = 131072
SLOW = 512
FAST = 256
HALF = SLOW // 2
KEPT = HALF + 8
DEVICES = 256
MIB = 1 << 20
FILTER_VMEM = 16 * MIB
GRAM_VMEM = 24 * MIB
FOLD_VMEM = 16 * MIB

EVERY = ("z", "yh", "yl", "x", "core")
ROWS = ("z", "yh")
TIMES = ("yl", "x", "core")
PLANE = ("yl", "x", "yh")

F32 = jnp.float32
BF16 = jnp.bfloat16


def split_table(table):
    upper = table.astype(np.float32).astype(BF16)
    lower = (table - upper.astype(np.float64)).astype(np.float32).astype(BF16)
    return upper, lower


def phase(rows, cols, length):
    index = np.outer(np.asarray(rows, np.int64), np.asarray(cols, np.int64)) % length
    return index * (2.0 * math.pi / length)


def host_tables():
    slow = np.arange(SLOW)
    cosine = np.cos(phase(np.arange(HALF + 1), slow, SLOW))
    sine = np.sin(phase(np.arange(1, HALF), slow, SLOW))
    real_fold = np.concatenate([cosine[:HALF], cosine[HALF:], -sine], axis=0)
    turn = phase(np.arange(KEPT), np.arange(FAST), EPOCHS)
    inner = phase(np.arange(FAST), np.arange(FAST), FAST)
    cosine, sine = np.cos(inner), np.sin(inner)
    inner = np.concatenate([cosine, sine - cosine, cosine + sine], axis=1)
    odd = 2 * np.arange(HALF) + 1
    spread = np.cos(phase(odd, odd, 8 * HALF)) * math.sqrt(2.0 / HALF)
    spread_upper, _ = split_table(spread)
    norm = math.sqrt(float((spread_upper.astype(np.float64)[0] ** 2).sum()))
    return (
        split_table(real_fold),
        (np.cos(turn).astype(np.float32), np.sin(turn).astype(np.float32)),
        split_table(inner),
        spread_upper,
        norm,
    )


def dot(left, right):
    return jnp.dot(left, right, preferred_element_type=F32)


def join(parts, axis):
    return jnp.concatenate(parts, axis=axis)


def settle_kernel(table_ref, after_ref, out_ref):
    del table_ref, after_ref, out_ref


def settle(table, after):
    return pl.pallas_call(
        settle_kernel,
        out_shape=jax.ShapeDtypeStruct(table.shape, table.dtype),
        in_specs=[pl.BlockSpec(memory_space=pl.ANY)] * 2,
        out_specs=pl.BlockSpec(memory_space=pl.ANY),
        input_output_aliases={0: 0},
        compiler_params=pltpu.CompilerParams(vmem_limit_bytes=FOLD_VMEM),
        name="settle",
    )(table, after)


def filter_kernel(
    series_ref,
    fold_ref,
    inner_ref,
    turn_ref,
    gain_ref,
    out_ref,
    lines_ref,
):
    fold_hi, fold_lo = fold_ref.at[0:SLOW], fold_ref.at[SLOW : 2 * SLOW]
    spread = fold_ref.at[2 * SLOW : 2 * SLOW + HALF]
    inner_hi, inner_lo = inner_ref.at[0:FAST], inner_ref.at[FAST : 2 * FAST]
    turn_cos, turn_sin = turn_ref.at[0:KEPT], turn_ref.at[KEPT : 2 * KEPT]
    blocks, columns, runs, _ = series_ref.shape
    first_row = lax.broadcasted_iota(jnp.int32, (HALF, FAST), 0) == 0
    gain = gain_ref[0:HALF, :]
    edge_gain = gain_ref[HALF : HALF + 1, :]
    tiles = 2 * FAST // 128
    for column in range(columns):
        series = join([series_ref[j, column] for j in range(blocks)], 0)
        folded = dot(join([fold_hi[...], fold_lo[...]], 1), join([series, series], 0))
        real = folded[0:HALF]
        imag = folded[HALF:SLOW]
        edge = imag[0:1]
        cosine = turn_cos[0:HALF, :]
        sine = turn_sin[0:HALF, :]
        turned_re = real * cosine + imag * sine
        turned_im = jnp.where(first_row, 0.0, imag * cosine - real * sine)
        edge_re = edge * turn_cos[HALF : HALF + 1, :]
        edge_im = -edge * turn_sin[HALF : HALF + 1, :]
        edge_re, edge_im = (jnp.broadcast_to(row, (16, FAST)) for row in (edge_re, edge_im))
        turned_re = join([turned_re, edge_re], 0)
        turned_im = join([turned_im, edge_im], 0)
        products = []
        for index, values in enumerate((turned_re + turned_im, turned_im, turned_re)):
            upper = values.astype(BF16)
            lower = (values - upper.astype(F32)).astype(BF16)
            lanes = slice(index * FAST, (index + 1) * FAST)
            table = join([inner_hi[:, lanes], inner_lo[:, lanes], inner_hi[:, lanes]], 0)
            products.append(dot(join([upper, upper, lower], 1), table))
        line_re = products[0] + products[1]
        line_im = products[0] - products[2]
        edge_line = (line_re[HALF : HALF + 1] + line_im[HALF : HALF + 1]) * edge_gain
        line_re = line_re[0:HALF] * gain
        line_im = line_im[0:HALF] * gain
        first = line_re + line_im
        line_re = jnp.where(first_row, first, line_re)
        line_im = jnp.where(first_row, jnp.broadcast_to(edge_line, (HALF, FAST)), line_im)
        packed = join([line_re, line_im], 1)
        upper = packed.astype(BF16)
        lower = (packed - upper.astype(F32)).astype(BF16)
        mixed = dot(spread[...], join([upper, lower], 0))
        for tile in range(tiles):
            lines_ref[pl.ds(column * tiles + tile, HALF, stride=columns * tiles), :] = mixed[
                :, tile * 128 : (tile + 1) * 128
            ]
    out_ref[...] = lines_ref[...].astype(BF16)


def filter_columns(series, tables, gain):
    rows = DEVICES * series.shape[1] * 2 * FAST // 128
    return pl.pallas_call(
        filter_kernel,
        out_shape=jax.ShapeDtypeStruct((rows, 128), BF16),
        scratch_shapes=[pltpu.VMEM((rows, 128), F32)],
        compiler_params=pltpu.CompilerParams(vmem_limit_bytes=FILTER_VMEM),
        cost_estimate=pl.CostEstimate(
            flops=2_000_000_000 * series.shape[1], bytes_accessed=4 * MIB, transcendentals=0
        ),
        name="filter",
    )(series, *tables, gain)


def half_gram(core_ref, ref):
    start = 64 * core_ref[0]
    left = [ref[pl.ds(pl.multiple_of(128 * b + start, 64), 64), :] for b in range(8)]
    right = [ref[64 * b : 64 * b + 64, :] for b in (*range(0, 16, 2), *range(1, 16, 2))]
    return lax.dot_general(
        join(left, 0), join(right, 0), (((1,), (1,)), ((), ())), preferred_element_type=F32
    )


def gram_mine_kernel(core_ref, mine_ref, out_ref):
    out_ref[...] = half_gram(core_ref, mine_ref)


def gram_other_kernel(core_ref, other_ref, begun_ref, out_ref):
    total = (begun_ref[...] + half_gram(core_ref, other_ref)).astype(BF16)
    for block in range(8):
        for parity in range(2):
            out_ref[2 * block + parity] = total[
                64 * block : 64 * block + 64, 512 * parity : 512 * parity + 512
            ]


def gram(kernel, shape, dtype, name, core, *arrays):
    return pl.pallas_call(
        kernel,
        out_shape=jax.ShapeDtypeStruct(shape, dtype),
        in_specs=[pl.BlockSpec(memory_space=pltpu.SMEM)]
        + [pl.BlockSpec(memory_space=pltpu.VMEM)] * len(arrays),
        compiler_params=pltpu.CompilerParams(vmem_limit_bytes=GRAM_VMEM),
        cost_estimate=pl.CostEstimate(
            flops=1_000_000_000, bytes_accessed=4 * MIB, transcendentals=0
        ),
        name=name,
    )(core, *arrays)


def fold_kernel(parts_ref, out_ref):
    total = parts_ref[0].astype(F32)
    for chip in range(1, parts_ref.shape[0]):
        total += parts_ref[chip].astype(F32)
    lane = lax.broadcasted_iota(jnp.int32, (32, 128), 1) < 64
    for pair in range(4):
        upper = total[0:32, pair * 128 : (pair + 1) * 128]
        lower = total[32:64, pair * 128 : (pair + 1) * 128]
        out_ref[2 * pair] = jnp.where(lane, upper, pltpu.roll(lower, 64, 1))
        out_ref[2 * pair + 1] = jnp.where(lane, pltpu.roll(upper, 64, 1), lower)


def fold(parts):
    return pl.pallas_call(
        fold_kernel,
        out_shape=jax.ShapeDtypeStruct((8, 32, 128), F32),
        compiler_params=pltpu.CompilerParams(vmem_limit_bytes=FOLD_VMEM),
        name="fold",
    )(parts)


def finish_kernel(parts_ref, out_ref):
    total = parts_ref[0]
    for part in range(1, parts_ref.shape[0]):
        total += parts_ref[part]
    block = join([total[:, 0:64], total[:, 64:128]], 0)
    out_ref[...] = block.T


def finish(parts):
    return pl.pallas_call(
        finish_kernel,
        out_shape=jax.ShapeDtypeStruct((64, 64), F32),
        compiler_params=pltpu.CompilerParams(vmem_limit_bytes=FOLD_VMEM),
        name="finish",
    )(parts)


def gain_table(response, norm):
    grid = response.reshape(FAST, SLOW)
    mirror = jnp.concatenate(
        [
            jnp.roll(jnp.flip(grid[:, 0:1], axis=0), 1, axis=0),
            jnp.flip(grid[:, HALF : SLOW], axis=(0, 1)),
        ],
        axis=1,
    )
    even = (grid[:, : HALF + 1] + mirror) * 0.5
    weight = np.full((1, HALF + 1), math.sqrt(2.0))
    weight[0, 0] = weight[0, HALF] = 1.0
    even = even * jnp.asarray((weight / (EPOCHS * norm)).astype(np.float32))
    return jnp.pad(even.T, ((0, KEPT - HALF - 1), (0, 0)))


def exchange(values, axes):
    return lax.all_to_all(values, axes, split_axis=0, concat_axis=0, tiled=True)


def on_device(panel, response):
    fold_tables, turn_tables, inner_tables, spread, norm = host_tables()
    tables = (
        [*fold_tables, np.concatenate([spread, spread], axis=1)],
        inner_tables,
        turn_tables,
    )
    tables = [jnp.asarray(np.concatenate(table)) for table in tables]
    gain = gain_table(response, norm)
    tables = tuple(settle(table, gain) for table in tables)
    tiles = 2 * FAST // 128
    columns = panel.shape[0] // 16
    series = exchange(panel.reshape(16, columns, -1, FAST), TIMES)
    lines = filter_columns(series, tables, gain)
    lines = exchange(lines.reshape(DEVICES, tiles * columns, 128), EVERY)
    mine = lines.reshape(DEVICES * columns, 2 * FAST)
    other = lax.ppermute(mine, "core", [(0, 1), (1, 0)])
    core = lax.axis_index("core").astype(jnp.int32).reshape(1)
    begun = gram(gram_mine_kernel, (512, 1024), F32, "gram_mine", core, mine)
    part = gram(gram_other_kernel, (16, 64, 512), BF16, "gram_other", core, other, begun)
    folded = exchange(fold(exchange(part, PLANE)), ("z",))
    return finish(folded)


def solution(mesh):
    fine = Mesh(mesh.devices.reshape(2, 4, 2, 8, 2), ("yl", "x", "core", "z", "yh"))
    return jax.shard_map(
        on_device,
        mesh=fine,
        in_specs=(P(ROWS, TIMES), P()),
        out_specs=P(ROWS, TIMES),
        check_vma=False,
    )
```

time: 119 us -> 112 us (0.941); the launches traced: 118 us -> 112 us
  local copies, waits for them, and re-layouts: 15.7 us -> 7.76 us
  waiting for transfers between devices: 5.24 us -> 11.6 us
  blocking collectives: 79.1 us -> 75.5 us
    all_to_all x1, waiting for transfers between devices: 3.34 us -> 9.7 us  [exchange(): return lax.all_to_all(values, axes, split_axis=0, concat_axis=0, tiled=True)]
    all_to_all x3, blocking collectives: 79.1 us -> 75.5 us  [exchange(): return lax.all_to_all(values, axes, split_axis=0, concat_axis=0, tiled=True)]
    rev x1, local copies, waits for them, and re-layouts: 3.12 us -> 0.37 us  [gain_table(): jnp.flip(grid[:, HALF:SLOW], axis=(0, 1))]
    unnamed x27 -> x17, local copies, waits for them, and re-layouts: 8.15 us -> 6.05 us
    slice x1, local copies, waits for them, and re-layouts: 1.91 us -> 0.04 us  [gain_table(): even = (grid[:, :HALF + 1] + mirror) * 0.5]
  transfers between devices with their start and end apart: 2 -> 2, of which waited for: 2 -> 2; matrix products, arithmetic and copies ran while one was open for 10% -> 3% of each run, Pallas kernels for 1% -> 1%
where the time goes in v3:
time: 112 us
  blocking collectives  75.5 us (67%)
  waiting for transfers between devices  11.6 us (10%)
  Pallas kernels  9.69 us (9%)
  local copies, waits for them, and re-layouts  7.76 us (7%)
  starting transfers between devices  6.5 us (6%)
    all_to_all x3, blocking collectives, exchange(): return lax.all_to_all(values, axes, split_axis=0, concat_axis=0, tiled=True)  75.5 us
    all_to_all x1, waiting for transfers between devices, exchange(): return lax.all_to_all(values, axes, split_axis=0, concat_axis=0, tiled=True)  9.7 us
    pallas_call x1, Pallas kernels, filter_columns(): pl.pallas_call(filter_kernel, out_shape=jax.ShapeDtypeStruct((rows, 128),...  7.22 us
    all_to_all x1, starting transfers between devices, exchange(): return lax.all_to_all(values, axes, split_axis=0, concat_axis=0, tiled=True)  6.41 us
    unnamed x17, local copies, waits for them, and re-layouts  6.05 us
  transfers between devices with their start and end apart: 2, of which 2 were waited for; matrix products, arithmetic and copies ran while one was open for 3% of the time, Pallas kernels for 1%

profile of v3, /device:TPU:8, one launch (start us, length us, event | category | flops | bytes accessed | tf_op | source)
XLA Modules:
  0.0 111.9 jit_solution(16156530909957074553)
XLA Ops:
  0.0 2.5 %copy.18 = bf16[8,8,32,256]{3,2,1,0:T(8,128)(2,1)} copy(bf16[8,8,32,256]{3,1,2,0:T(8,128)(2,1)} %bitcast.10) | data formatting | bytes 2097152
  2.5 6.4 %all-to-all-start = ((bf16[16,4,32,256]{3,2,1,0:T(8,128)(2,1)}), bf16[16,4,32,256]{3,2,1,0:T(8,128)(2,1)}, u32[]{:S(2)}, u32[]{:S(2)}) async-start(bf16[16,4,32,256]{3,2,1,0:T(8,128)(2,1)} %bitcast.6), calls=%async_computation | async-start | bytes 2097152 | tf_op jit(solution)/shard_map/all_to_all | solution.py:253
  8.9 0.0 copy-done.2
  8.9 0.0 copy-start
  9.0 0.1 reshape.19
  9.1 0.5 slice.27
  9.7 0.6 copy-done
  10.3 0.1 copy.25.table_ref
  10.4 0.1 copy.14
  10.5 0.0 copy-start.3
  10.5 0.1 copy.17
  10.6 0.4 rev.6
  11.0 0.1 copy.16
  11.1 0.2 reverse.2
  11.3 0.1 slice.30
  11.4 1.1 %copy.26.table_ref = bf16[512,768]{1,0:T(8,128)(2,1)S(1)} copy(bf16[512,768]{1,0:T(8,128)(2,1)} %constant.20.clone) | data formatting | bytes 1572864
  12.5 0.0 copy-done.3
  12.5 0.8 fusion.1
  13.3 0.0 copy-start.1
  13.3 1.0 copy-done.1
  14.4 9.7 %all-to-all-done.series_ref = bf16[16,4,32,256]{3,2,1,0:T(8,128)(2,1)} async-done(((bf16[16,4,32,256]{3,2,1,0:T(8,128)(2,1)}), bf16[16,4,32,256]{3,2,1,0:T(8,128)(2,1)}, u32[]{:S(2)}, u32[]{:S(2)}) %all-to-all-start) | async-done | bytes 1048608 | tf_op jit(solution)/shard_map/all_to_all | solution.py:253
  24.1 7.2 %filter.1 = bf16[4096,128]{1,0:T(8,128)(2,1)S(1)} custom-call(bf16[16,4,32,256]{3,2,1,0:T(8,128)(2,1)} %all-to-all-done.series_ref, bf16[1280,512]{1,0:T(8,128)(2,1)S(1)} %settle.3.fold_ref, bf16[512,768]{1,0:T(8,128)(2,1)S(1)} %settle.4.inner_ref, f32[528,256]{1,0:T(8,128)S(1)} %settle.5.turn_ref, f32[264,256]{1,0:T(8,128)S(1)} %pad.4.after_ref.gain_ref), custom_call_target="tpu_custom_call" | custom-call | flops 8000000000 | bytes 4194304 | tf_op jit(solution)/shard_map/filter/pallas_call | solution.py:150
  31.3 43.5 %all_to_all.20 = bf16[256,16,128]{2,1,0:T(8,128)(2,1)S(1)} all-to-all(bf16[256,16,128]{2,1,0:T(8,128)(2,1)S(1)} %bitcast.9), channel_id=1, replica_groups=mesh['yl'=2,'x'=4,'core'=2,'z'=8,'yh'=2] {'z','yh','yl','x','core'}, dimensions={0} | all-to-all | bytes 2097152 | tf_op jit(solution)/shard_map/all_to_all | solution.py:253
  74.8 0.6 reshape.21.mine_ref
  75.5 0.1 collective-permute-start
  75.6 0.7 gram_mine.1.begun_ref
  76.3 1.9 %collective-permute-done.other_ref = bf16[1024,512]{1,0:T(8,128)(2,1)S(1)} collective-permute-done((bf16[1024,512]{1,0:T(8,128)(2,1)S(1)}, bf16[1024,512]{1,0:T(8,128)(2,1)S(1)}, u32[]{:S(2)}, u32[]{:S(2)}) %collective-permute-start) | collective-permute-done | bytes 1048608 | tf_op jit(solution)/shard_map/ppermute | solution.py:272
  78.2 0.7 gram_other.1
  79.0 20.5 %all_to_all.21.parts_ref = bf16[16,64,512]{2,1,0:T(8,128)(2,1)S(1)} all-to-all(bf16[16,64,512]{2,1,0:T(8,128)(2,1)S(1)} %gram_other.1), channel_id=1, replica_groups=mesh['yl'=2,'x'=4,'core'=2,'z'=8,'yh'=2] {'yl','x','yh'}, dimensions={0} | all-to-all | bytes 2097152 | tf_op jit(solution)/shard_map/all_to_all | solution.py:253
  99.5 0.2 fold.1
  99.7 11.5 %all_to_all.22.parts_ref = f32[8,32,128]{2,1,0:T(8,128)S(1)} all-to-all(f32[8,32,128]{2,1,0:T(8,128)S(1)} %fold.1), channel_id=1, replica_groups=mesh['yl'=2,'x'=4,'core'=2,'z'=8,'yh'=2] {'z'}, dimensions={0} | all-to-all | bytes 262144 | tf_op jit(solution)/shard_map/all_to_all | solution.py:253
  111.2 0.8 finish.1
  (9 shorter events, 0.1 us)
Async XLA Ops:
  2.5 6.4 %copy-start.2 = (f32[131072]{0:T(1024)S(1)}, f32[131072]{0:T(1024)}, u32[]{:S(2)}) copy-start(f32[131072]{0:T(1024)} %param.7) | copy-start | bytes 1572868
  2.5 21.6 %all-to-all-start = ((bf16[16,4,32,256]{3,2,1,0:T(8,128)(2,1)}), bf16[16,4,32,256]{3,2,1,0:T(8,128)(2,1)}, u32[]{:S(2)}, u32[]{:S(2)}) async-start(bf16[16,4,32,256]{3,2,1,0:T(8,128)(2,1)} %bitcast.6), calls=%async_computation | async-start | bytes 2097152 | tf_op jit(solution)/shard_map/all_to_all | solution.py:253
  8.9 1.3 %copy-start = (bf16[1280,512]{1,0:T(8,128)(2,1)S(1)}, bf16[1280,512]{1,0:T(8,128)(2,1)}, u32[]{:S(2)}) copy-start(bf16[1280,512]{1,0:T(8,128)(2,1)} %constant.19.clone) | copy-start | bytes 3932164
  10.5 2.0 %copy-start.3 = (f32[257]{0:T(512)S(1)}, f32[257]{0:T(512)}, u32[]{:S(2)}) copy-start(f32[257]{0:T(512)} %constant.26) | copy-start | bytes 3088
  13.3 1.1 copy-start.1
  75.5 2.7 %collective-permute-start = (bf16[1024,512]{1,0:T(8,128)(2,1)S(1)}, bf16[1024,512]{1,0:T(8,128)(2,1)S(1)}, u32[]{:S(2)}, u32[]{:S(2)}) collective-permute-start(bf16[1024,512]{1,0:T(8,128)(2,1)S(1)} %reshape.21.mine_ref), channel_id=1, source_target_pairs={{0,16},{16,0},{1,17},{17,1},{2,18},{18,2},{3,19},{19,3},{4,20},{20... | collective-permute-start | bytes 3145736 | tf_op jit(solution)/shard_map/ppermute | solution.py:272

commit v4 on v3

--- a/solution.py
+++ b/solution.py
@@ -16,23 +16,29 @@
 KEPT = HALF + 8
 DEVICES = 256
 MIB = 1 << 20
-FILTER_VMEM = 16 * MIB
+FILTER_VMEM = 10 * MIB
 GRAM_VMEM = 24 * MIB
 FOLD_VMEM = 16 * MIB
 
 EVERY = ("z", "yh", "yl", "x", "core")
 ROWS = ("z", "yh")
 TIMES = ("yl", "x", "core")
-PLANE = ("yl", "x", "yh")
+PLANE = ("yh", "yl", "x")
 
 F32 = jnp.float32
 BF16 = jnp.bfloat16
+F8 = jnp.float8_e5m2
+SHIFT = 256.0
 
 
 def split_table(table):
     upper = table.astype(np.float32).astype(BF16)
     lower = (table - upper.astype(np.float64)).astype(np.float32).astype(BF16)
     return upper, lower
+
+
+def coarse(table):
+    return np.asarray(table, np.float32).astype(F8)
 
 
 def phase(rows, cols, length):
@@ -81,7 +87,7 @@
         in_specs=[pl.BlockSpec(memory_space=pl.ANY)] * 2,
         out_specs=pl.BlockSpec(memory_space=pl.ANY),
         input_output_aliases={0: 0},
-        compiler_params=pltpu.CompilerParams(vmem_limit_bytes=FOLD_VMEM),
+        compiler_params=pltpu.CompilerParams(vmem_limit_bytes=MIB),
         name="settle",
     )(table, after)
 
@@ -90,14 +96,17 @@
     series_ref,
     fold_ref,
     inner_ref,
+    coarse_ref,
+    rest_ref,
     turn_ref,
     gain_ref,
     out_ref,
     lines_ref,
 ):
-    fold_hi, fold_lo = fold_ref.at[0:SLOW], fold_ref.at[SLOW : 2 * SLOW]
-    spread = fold_ref.at[2 * SLOW : 2 * SLOW + HALF]
-    inner_hi, inner_lo = inner_ref.at[0:FAST], inner_ref.at[FAST : 2 * FAST]
+    fold_hi, fold_lo = fold_ref, coarse_ref.at[0:SLOW]
+    spread, spread_lo = inner_ref.at[:, 0:FAST], coarse_ref.at[SLOW : SLOW + HALF, 0:FAST]
+    inner_hi = inner_ref.at[:, FAST : 4 * FAST]
+    inner_lo = rest_ref
     turn_cos, turn_sin = turn_ref.at[0:KEPT], turn_ref.at[KEPT : 2 * KEPT]
     blocks, columns, runs, _ = series_ref.shape
     first_row = lax.broadcasted_iota(jnp.int32, (HALF, FAST), 0) == 0
@@ -106,7 +115,8 @@
     tiles = 2 * FAST // 128
     for column in range(columns):
         series = join([series_ref[j, column] for j in range(blocks)], 0)
-        folded = dot(join([fold_hi[...], fold_lo[...]], 1), join([series, series], 0))
+        folded = dot(fold_hi[...], series)
+        folded += dot(fold_lo[...], series.astype(F32).astype(F8)) * (1 / SHIFT)
         real = folded[0:HALF]
         imag = folded[HALF:SLOW]
         edge = imag[0:1]
@@ -122,10 +132,11 @@
         products = []
         for index, values in enumerate((turned_re + turned_im, turned_im, turned_re)):
             upper = values.astype(BF16)
-            lower = (values - upper.astype(F32)).astype(BF16)
+            lower = ((values - upper.astype(F32)) * SHIFT).astype(F8)
             lanes = slice(index * FAST, (index + 1) * FAST)
-            table = join([inner_hi[:, lanes], inner_lo[:, lanes], inner_hi[:, lanes]], 0)
-            products.append(dot(join([upper, upper, lower], 1), table))
+            product = dot(upper, inner_hi[:, lanes])
+            coarse_values = join([upper.astype(F32).astype(F8), lower], 1)
+            products.append(product + dot(coarse_values, inner_lo[:, lanes]) * (1 / SHIFT))
         line_re = products[0] + products[1]
         line_im = products[0] - products[2]
         edge_line = (line_re[HALF : HALF + 1] + line_im[HALF : HALF + 1]) * edge_gain
@@ -136,8 +147,8 @@
         line_im = jnp.where(first_row, jnp.broadcast_to(edge_line, (HALF, FAST)), line_im)
         packed = join([line_re, line_im], 1)
         upper = packed.astype(BF16)
-        lower = (packed - upper.astype(F32)).astype(BF16)
-        mixed = dot(spread[...], join([upper, lower], 0))
+        lower = ((packed - upper.astype(F32)) * SHIFT).astype(F8)
+        mixed = dot(spread[...], upper) + dot(spread_lo[...], lower) * (1 / SHIFT)
         for tile in range(tiles):
             lines_ref[pl.ds(column * tiles + tile, HALF, stride=columns * tiles), :] = mixed[
                 :, tile * 128 : (tile + 1) * 128
@@ -176,7 +187,7 @@
     total = (begun_ref[...] + half_gram(core_ref, other_ref)).astype(BF16)
     for block in range(8):
         for parity in range(2):
-            out_ref[2 * block + parity] = total[
+            out_ref[8 * parity + block] = total[
                 64 * block : 64 * block + 64, 512 * parity : 512 * parity + 512
             ]
 
@@ -255,12 +266,15 @@
 
 def on_device(panel, response):
     fold_tables, turn_tables, inner_tables, spread, norm = host_tables()
+    (fold_hi, fold_lo), (inner_hi, inner_lo) = fold_tables, inner_tables
     tables = (
-        [*fold_tables, np.concatenate([spread, spread], axis=1)],
-        inner_tables,
-        turn_tables,
-    )
-    tables = [jnp.asarray(np.concatenate(table)) for table in tables]
+        fold_hi,
+        np.concatenate([spread, inner_hi], axis=1),
+        np.concatenate([coarse(np.asarray(fold_lo, np.float32) * SHIFT), np.tile(coarse(spread), (1, 2))]),
+        np.concatenate([coarse(np.asarray(inner_lo, np.float32) * SHIFT), coarse(inner_hi)]),
+        np.concatenate(turn_tables),
+    )
+    tables = [jnp.asarray(table) for table in tables]
     gain = gain_table(response, norm)
     tables = tuple(settle(table, gain) for table in tables)
     tiles = 2 * FAST // 128

time: 112 us -> 111 us (level); the launches traced: 112 us -> 110 us
  local copies, waits for them, and re-layouts: 7.76 us -> 6.2 us
  waiting for transfers between devices: 11.6 us -> 13.1 us
  Pallas kernels: 9.69 us -> 8.56 us
    unnamed x17 -> x25, local copies, waits for them, and re-layouts: 6.05 us -> 4.49 us
    all_to_all x1, waiting for transfers between devices: 9.7 us -> 11.2 us  [exchange(): return lax.all_to_all(values, axes, split_axis=0, concat_axis=0, tiled=True)]
    pallas_call x1, Pallas kernels: 7.22 us -> 6.06 us  [filter_columns(): pl.pallas_call(filter_kernel, out_shape=jax.ShapeDtypeStruct((rows, 128),...]
  transfers between devices with their start and end apart: 2 -> 2, of which waited for: 2 -> 2; matrix products, arithmetic and copies ran while one was open for 3% -> 2% of each run, Pallas kernels for 1% -> 1%
where the time goes in v4:
time: 111 us; the launch traced here: 110 us
  blocking collectives  74.4 us (67%)
  waiting for transfers between devices  13.1 us (12%)
  Pallas kernels  8.56 us (8%)
  starting transfers between devices  6.49 us (6%)
  local copies, waits for them, and re-layouts  6.2 us (6%)
    all_to_all x3, blocking collectives, exchange(): return lax.all_to_all(values, axes, split_axis=0, concat_axis=0, tiled=True)  74.4 us
    all_to_all x1, waiting for transfers between devices, exchange(): return lax.all_to_all(values, axes, split_axis=0, concat_axis=0, tiled=True)  11.2 us
    all_to_all x1, starting transfers between devices, exchange(): return lax.all_to_all(values, axes, split_axis=0, concat_axis=0, tiled=True)  6.4 us
    pallas_call x1, Pallas kernels, filter_columns(): pl.pallas_call(filter_kernel, out_shape=jax.ShapeDtypeStruct((rows, 128),...  6.06 us
    unnamed x25, local copies, waits for them, and re-layouts  4.49 us
  transfers between devices with their start and end apart: 2, of which 2 were waited for; matrix products, arithmetic and copies ran while one was open for 2% of the time, Pallas kernels for 1%

profile of v4, /device:TPU:8, one launch (start us, length us, event | category | flops | bytes accessed | tf_op | source)
XLA Modules:
  0.0 109.7 jit_solution(4577153146360868303)
XLA Ops:
  0.0 2.6 %copy.22 = bf16[8,8,32,256]{3,2,1,0:T(8,128)(2,1)} copy(bf16[8,8,32,256]{3,1,2,0:T(8,128)(2,1)} %bitcast.10) | data formatting | bytes 2097152
  2.6 6.4 %all-to-all-start = ((bf16[16,4,32,256]{3,2,1,0:T(8,128)(2,1)}), bf16[16,4,32,256]{3,2,1,0:T(8,128)(2,1)}, u32[]{:S(2)}, u32[]{:S(2)}) async-start(bf16[16,4,32,256]{3,2,1,0:T(8,128)(2,1)} %bitcast.6), calls=%async_computation | async-start | bytes 2097152 | tf_op jit(solution)/shard_map/all_to_all | solution.py:264
  9.0 0.1 reshape.19
  9.1 0.0 copy-start.2
  9.1 0.0 copy-start.6
  9.2 0.5 slice.27
  9.7 0.1 copy.18
  9.9 0.1 copy.21
  10.0 0.4 rev.6
  10.4 0.1 copy.20
  10.5 0.2 reverse.2
  10.7 0.1 slice.30
  10.8 0.0 copy-start.5
  10.8 0.8 fusion.1
  11.6 0.0 copy-start.4
  11.7 0.1 copy-done.5
  11.8 0.1 copy.35.table_ref
  11.9 0.8 copy-done.4
  12.7 0.1 copy.36.table_ref
  12.7 0.1 copy-done
  12.9 11.2 %all-to-all-done.series_ref = bf16[16,4,32,256]{3,2,1,0:T(8,128)(2,1)} async-done(((bf16[16,4,32,256]{3,2,1,0:T(8,128)(2,1)}), bf16[16,4,32,256]{3,2,1,0:T(8,128)(2,1)}, u32[]{:S(2)}, u32[]{:S(2)}) %all-to-all-start) | async-done | bytes 1048608 | tf_op jit(solution)/shard_map/all_to_all | solution.py:264
  24.1 6.1 %filter.1 = bf16[4096,128]{1,0:T(8,128)(2,1)S(1)} custom-call(bf16[16,4,32,256]{3,2,1,0:T(8,128)(2,1)} %all-to-all-done.series_ref, bf16[512,512]{1,0:T(8,128)(2,1)S(1)} %settle.5.fold_ref, bf16[256,1024]{1,0:T(8,128)(2,1)S(1)} %settle.6.inner_ref, f8e5m2[768,512]{1,0:T(32,128)(4,1)S(1)} %settle.7.coarse_ref, f8e5m2[512,768]{1,0:T(32,128)(4,1)S(1)} %settle.8.rest_ref, ...), custom_call_target="tpu_custom_call" | custom-call | flops 8000000000 | bytes 4194304 | tf_op jit(solution)/shard_map/filter/pallas_call | solution.py:161
  30.2 43.5 %all_to_all.20 = bf16[256,16,128]{2,1,0:T(8,128)(2,1)S(1)} all-to-all(bf16[256,16,128]{2,1,0:T(8,128)(2,1)S(1)} %bitcast.9), channel_id=1, replica_groups=mesh['yl'=2,'x'=4,'core'=2,'z'=8,'yh'=2] {'z','yh','yl','x','core'}, dimensions={0} | all-to-all | bytes 2097152 | tf_op jit(solution)/shard_map/all_to_all | solution.py:264
  73.7 0.6 reshape.21.mine_ref
  74.3 0.1 collective-permute-start
  74.4 0.7 gram_mine.1.begun_ref
  75.2 1.9 %collective-permute-done.other_ref = bf16[1024,512]{1,0:T(8,128)(2,1)S(1)} collective-permute-done((bf16[1024,512]{1,0:T(8,128)(2,1)S(1)}, bf16[1024,512]{1,0:T(8,128)(2,1)S(1)}, u32[]{:S(2)}, u32[]{:S(2)}) %collective-permute-start) | collective-permute-done | bytes 1048608 | tf_op jit(solution)/shard_map/ppermute | solution.py:286
  77.1 0.8 gram_other.1
  77.9 19.4 %all_to_all.21.parts_ref = bf16[16,64,512]{2,1,0:T(8,128)(2,1)S(1)} all-to-all(bf16[16,64,512]{2,1,0:T(8,128)(2,1)S(1)} %gram_other.1), channel_id=1, replica_groups=mesh['yl'=2,'x'=4,'core'=2,'z'=8,'yh'=2] {'yh','yl','x'}, dimensions={0} | all-to-all | bytes 2097152 | tf_op jit(solution)/shard_map/all_to_all | solution.py:264
  97.3 0.2 fold.1
  97.5 11.5 %all_to_all.22.parts_ref = f32[8,32,128]{2,1,0:T(8,128)S(1)} all-to-all(f32[8,32,128]{2,1,0:T(8,128)S(1)} %fold.1), channel_id=1, replica_groups=mesh['yl'=2,'x'=4,'core'=2,'z'=8,'yh'=2] {'z'}, dimensions={0} | all-to-all | bytes 262144 | tf_op jit(solution)/shard_map/all_to_all | solution.py:264
  109.0 0.8 finish.1
  (19 shorter events, 0.2 us)
Async XLA Ops:
  0.0 9.0 %copy-start.1 = (f32[131072]{0:T(1024)S(1)}, f32[131072]{0:T(1024)}, u32[]{:S(2)}) copy-start(f32[131072]{0:T(1024)} %param.9) | copy-start | bytes 1572868
  2.6 7.1 %copy-start.3 = (bf16[512,512]{1,0:T(8,128)(2,1)S(1)}, bf16[512,512]{1,0:T(8,128)(2,1)}, u32[]{:S(2)}) copy-start(bf16[512,512]{1,0:T(8,128)(2,1)} %constant.23.clone) | copy-start | bytes 1572868
  2.6 21.6 %all-to-all-start = ((bf16[16,4,32,256]{3,2,1,0:T(8,128)(2,1)}), bf16[16,4,32,256]{3,2,1,0:T(8,128)(2,1)}, u32[]{:S(2)}, u32[]{:S(2)}) async-start(bf16[16,4,32,256]{3,2,1,0:T(8,128)(2,1)} %bitcast.6), calls=%async_computation | async-start | bytes 2097152 | tf_op jit(solution)/shard_map/all_to_all | solution.py:264
  9.1 1.7 %copy-start.2 = (bf16[256,1024]{1,0:T(8,128)(2,1)S(1)}, bf16[256,1024]{1,0:T(8,128)(2,1)}, u32[]{:S(2)}) copy-start(bf16[256,1024]{1,0:T(8,128)(2,1)} %constant.24.clone) | copy-start | bytes 1572868
  9.1 1.7 %copy-start.6 = (f32[257]{0:T(512)S(1)}, f32[257]{0:T(512)}, u32[]{:S(2)}) copy-start(f32[257]{0:T(512)} %constant.32) | copy-start | bytes 3088
  10.8 1.0 copy-start.5
  11.6 1.0 copy-start.4
  11.8 1.1 copy-start
  74.3 2.7 %collective-permute-start = (bf16[1024,512]{1,0:T(8,128)(2,1)S(1)}, bf16[1024,512]{1,0:T(8,128)(2,1)S(1)}, u32[]{:S(2)}, u32[]{:S(2)}) collective-permute-start(bf16[1024,512]{1,0:T(8,128)(2,1)S(1)} %reshape.21.mine_ref), channel_id=1, source_target_pairs={{0,16},{16,0},{1,17},{17,1},{2,18},{18,2},{3,19},{19,3},{4,20},{20... | collective-permute-start | bytes 3145736 | tf_op jit(solution)/shard_map/ppermute | solution.py:286

commit v5 on v4

--- a/solution.py
+++ b/solution.py
@@ -23,7 +23,7 @@
 EVERY = ("z", "yh", "yl", "x", "core")
 ROWS = ("z", "yh")
 TIMES = ("yl", "x", "core")
-PLANE = ("yh", "yl", "x")
+PLANE = ("yh", "x", "yl")
 
 F32 = jnp.float32
 BF16 = jnp.bfloat16
@@ -101,7 +101,6 @@
     turn_ref,
     gain_ref,
     out_ref,
-    lines_ref,
 ):
     fold_hi, fold_lo = fold_ref, coarse_ref.at[0:SLOW]
     spread, spread_lo = inner_ref.at[:, 0:FAST], coarse_ref.at[SLOW : SLOW + HALF, 0:FAST]
@@ -112,11 +111,10 @@
     first_row = lax.broadcasted_iota(jnp.int32, (HALF, FAST), 0) == 0
     gain = gain_ref[0:HALF, :]
     edge_gain = gain_ref[HALF : HALF + 1, :]
-    tiles = 2 * FAST // 128
     for column in range(columns):
         series = join([series_ref[j, column] for j in range(blocks)], 0)
         folded = dot(fold_hi[...], series)
-        folded += dot(fold_lo[...], series.astype(F32).astype(F8)) * (1 / SHIFT)
+        folded += dot(fold_lo[...], series.astype(F8)) * (1 / SHIFT)
         real = folded[0:HALF]
         imag = folded[HALF:SLOW]
         edge = imag[0:1]
@@ -135,7 +133,7 @@
             lower = ((values - upper.astype(F32)) * SHIFT).astype(F8)
             lanes = slice(index * FAST, (index + 1) * FAST)
             product = dot(upper, inner_hi[:, lanes])
-            coarse_values = join([upper.astype(F32).astype(F8), lower], 1)
+            coarse_values = join([values.astype(F8), lower], 1)
             products.append(product + dot(coarse_values, inner_lo[:, lanes]) * (1 / SHIFT))
         line_re = products[0] + products[1]
         line_im = products[0] - products[2]
@@ -149,19 +147,15 @@
         upper = packed.astype(BF16)
         lower = ((packed - upper.astype(F32)) * SHIFT).astype(F8)
         mixed = dot(spread[...], upper) + dot(spread_lo[...], lower) * (1 / SHIFT)
-        for tile in range(tiles):
-            lines_ref[pl.ds(column * tiles + tile, HALF, stride=columns * tiles), :] = mixed[
-                :, tile * 128 : (tile + 1) * 128
-            ]
-    out_ref[...] = lines_ref[...].astype(BF16)
+        out_ref[:, 2 * FAST * column : 2 * FAST * (column + 1)] = mixed.astype(BF16)
 
 
 def filter_columns(series, tables, gain):
-    rows = DEVICES * series.shape[1] * 2 * FAST // 128
     return pl.pallas_call(
         filter_kernel,
-        out_shape=jax.ShapeDtypeStruct((rows, 128), BF16),
-        scratch_shapes=[pltpu.VMEM((rows, 128), F32)],
+        out_shape=jax.ShapeDtypeStruct((DEVICES, series.shape[1] * 2 * FAST), BF16),
+        in_specs=[pl.BlockSpec(memory_space=pltpu.VMEM)] * (len(tables) + 2),
+        out_specs=pl.BlockSpec(memory_space=pltpu.VMEM),
         compiler_params=pltpu.CompilerParams(vmem_limit_bytes=FILTER_VMEM),
         cost_estimate=pl.CostEstimate(
             flops=2_000_000_000 * series.shape[1], bytes_accessed=4 * MIB, transcendentals=0
@@ -187,7 +181,7 @@
     total = (begun_ref[...] + half_gram(core_ref, other_ref)).astype(BF16)
     for block in range(8):
         for parity in range(2):
-            out_ref[8 * parity + block] = total[
+            out_ref[8 * parity + 2 * (block % 4) + block // 4] = total[
                 64 * block : 64 * block + 64, 512 * parity : 512 * parity + 512
             ]
 
@@ -198,6 +192,7 @@
         out_shape=jax.ShapeDtypeStruct(shape, dtype),
         in_specs=[pl.BlockSpec(memory_space=pltpu.SMEM)]
         + [pl.BlockSpec(memory_space=pltpu.VMEM)] * len(arrays),
+        out_specs=pl.BlockSpec(memory_space=pltpu.VMEM),
         compiler_params=pltpu.CompilerParams(vmem_limit_bytes=GRAM_VMEM),
         cost_estimate=pl.CostEstimate(
             flops=1_000_000_000, bytes_accessed=4 * MIB, transcendentals=0
@@ -222,6 +217,8 @@
     return pl.pallas_call(
         fold_kernel,
         out_shape=jax.ShapeDtypeStruct((8, 32, 128), F32),
+        in_specs=[pl.BlockSpec(memory_space=pltpu.VMEM)],
+        out_specs=pl.BlockSpec(memory_space=pltpu.VMEM),
         compiler_params=pltpu.CompilerParams(vmem_limit_bytes=FOLD_VMEM),
         name="fold",
     )(parts)
@@ -239,6 +236,8 @@
     return pl.pallas_call(
         finish_kernel,
         out_shape=jax.ShapeDtypeStruct((64, 64), F32),
+        in_specs=[pl.BlockSpec(memory_space=pltpu.VMEM)],
+        out_specs=pl.BlockSpec(memory_space=pltpu.VMEM),
         compiler_params=pltpu.CompilerParams(vmem_limit_bytes=FOLD_VMEM),
         name="finish",
     )(parts)

time: 111 us -> 111 us (level)
    all_to_all x3, blocking collectives: 74.4 us -> 75.5 us  [exchange(): return lax.all_to_all(values, axes, split_axis=0, concat_axis=0, tiled=True)]
    unnamed x25 -> x26, local copies, waits for them, and re-layouts: 4.49 us -> 4.72 us
where the time goes in v5:
time: 111 us
  blocking collectives  75.5 us (68%)
  waiting for transfers between devices  13.1 us (12%)
  Pallas kernels  8.04 us (7%)
  starting transfers between devices  6.49 us (6%)
  local copies, waits for them, and re-layouts  6.42 us (6%)
    all_to_all x3, blocking collectives, exchange(): return lax.all_to_all(values, axes, split_axis=0, concat_axis=0, tiled=True)  75.5 us
    all_to_all x1, waiting for transfers between devices, exchange(): return lax.all_to_all(values, axes, split_axis=0, concat_axis=0, tiled=True)  11.2 us
    all_to_all x1, starting transfers between devices, exchange(): return lax.all_to_all(values, axes, split_axis=0, concat_axis=0, tiled=True)  6.4 us
    pallas_call x1, Pallas kernels, filter_columns(): pl.pallas_call(filter_kernel, out_shape=jax.ShapeDtypeStruct((DEVICES, se...  5.54 us
    unnamed x26, local copies, waits for them, and re-layouts  4.72 us
  transfers between devices with their start and end apart: 2, of which 2 were waited for; matrix products, arithmetic and copies ran while one was open for 2% of the time, Pallas kernels for 1%

profile of v5, /device:TPU:8, one launch (start us, length us, event | category | flops | bytes accessed | tf_op | source)
XLA Modules:
  0.0 110.6 jit_solution(3692448412188452982)
XLA Ops:
  0.0 2.6 %copy.22 = bf16[8,8,32,256]{3,2,1,0:T(8,128)(2,1)} copy(bf16[8,8,32,256]{3,1,2,0:T(8,128)(2,1)} %bitcast.12) | data formatting | bytes 2097152
  2.6 6.4 %all-to-all-start = ((bf16[16,4,32,256]{3,2,1,0:T(8,128)(2,1)}), bf16[16,4,32,256]{3,2,1,0:T(8,128)(2,1)}, u32[]{:S(2)}, u32[]{:S(2)}) async-start(bf16[16,4,32,256]{3,2,1,0:T(8,128)(2,1)} %bitcast.5), calls=%async_computation | async-start | bytes 2097152 | tf_op jit(solution)/shard_map/all_to_all | solution.py:263
  9.0 0.1 reshape.19
  9.1 0.0 copy-start.2
  9.1 0.0 copy-start.6
  9.2 0.5 slice.27
  9.7 0.1 copy.18
  9.9 0.1 copy.21
  10.0 0.4 rev.6
  10.4 0.1 copy.20
  10.5 0.2 reverse.2
  10.7 0.1 slice.30
  10.8 0.0 copy-start.5
  10.8 0.8 fusion.1
  11.7 0.1 copy-done.5
  11.8 0.1 copy.36.table_ref
  11.9 0.8 copy-done.4
  12.7 0.1 copy.37.table_ref
  12.7 0.1 copy-done
  12.9 11.2 %all-to-all-done.series_ref = bf16[16,4,32,256]{3,2,1,0:T(8,128)(2,1)} async-done(((bf16[16,4,32,256]{3,2,1,0:T(8,128)(2,1)}), bf16[16,4,32,256]{3,2,1,0:T(8,128)(2,1)}, u32[]{:S(2)}, u32[]{:S(2)}) %all-to-all-start) | async-done | bytes 1048608 | tf_op jit(solution)/shard_map/all_to_all | solution.py:263
  24.1 5.5 %filter.1 = bf16[256,2048]{1,0:T(8,128)(2,1)S(1)} custom-call(bf16[16,4,32,256]{3,2,1,0:T(8,128)(2,1)} %all-to-all-done.series_ref, bf16[512,512]{1,0:T(8,128)(2,1)S(1)} %settle.5.fold_ref, bf16[256,1024]{1,0:T(8,128)(2,1)S(1)} %settle.6.inner_ref, f8e5m2[768,512]{1,0:T(32,128)(4,1)S(1)} %settle.7.coarse_ref, f8e5m2[512,768]{1,0:T(32,128)(4,1)S(1)} %settle.8.rest_ref, ...), custom_call_target="tpu_custom_call" | custom-call | flops 8000000000 | bytes 4194304 | tf_op jit(solution)/shard_map/filter/pallas_call | solution.py:154
  29.7 0.2 copy.23
  29.9 43.5 %all_to_all.20 = bf16[256,16,128]{2,1,0:T(8,128)(2,1)S(1)} all-to-all(bf16[256,16,128]{2,1,0:T(8,128)(2,1)S(1)} %bitcast.11), channel_id=1, replica_groups=mesh['yl'=2,'x'=4,'core'=2,'z'=8,'yh'=2] {'z','yh','yl','x','core'}, dimensions={0} | all-to-all | bytes 2097152 | tf_op jit(solution)/shard_map/all_to_all | solution.py:263
  73.4 0.6 reshape.21.mine_ref
  74.1 0.1 collective-permute-start
  74.2 0.7 gram_mine.1.begun_ref
  74.9 1.9 %collective-permute-done.other_ref = bf16[1024,512]{1,0:T(8,128)(2,1)S(1)} collective-permute-done((bf16[1024,512]{1,0:T(8,128)(2,1)S(1)}, bf16[1024,512]{1,0:T(8,128)(2,1)S(1)}, u32[]{:S(2)}, u32[]{:S(2)}) %collective-permute-start) | collective-permute-done | bytes 1048608 | tf_op jit(solution)/shard_map/ppermute | solution.py:285
  76.8 0.8 gram_other.1
  77.6 20.6 %all_to_all.21.parts_ref = bf16[16,64,512]{2,1,0:T(8,128)(2,1)S(1)} all-to-all(bf16[16,64,512]{2,1,0:T(8,128)(2,1)S(1)} %gram_other.1), channel_id=1, replica_groups=mesh['yl'=2,'x'=4,'core'=2,'z'=8,'yh'=2] {'yh','x','yl'}, dimensions={0} | all-to-all | bytes 2097152 | tf_op jit(solution)/shard_map/all_to_all | solution.py:263
  98.2 0.2 fold.1
  98.4 11.5 %all_to_all.22.parts_ref = f32[8,32,128]{2,1,0:T(8,128)S(1)} all-to-all(f32[8,32,128]{2,1,0:T(8,128)S(1)} %fold.1), channel_id=1, replica_groups=mesh['yl'=2,'x'=4,'core'=2,'z'=8,'yh'=2] {'z'}, dimensions={0} | all-to-all | bytes 262144 | tf_op jit(solution)/shard_map/all_to_all | solution.py:263
  109.8 0.8 finish.1
  (20 shorter events, 0.2 us)
Async XLA Ops:
  0.0 9.0 %copy-start.1 = (f32[131072]{0:T(1024)S(1)}, f32[131072]{0:T(1024)}, u32[]{:S(2)}) copy-start(f32[131072]{0:T(1024)} %param.9) | copy-start | bytes 1572868
  2.6 7.1 %copy-start.3 = (bf16[512,512]{1,0:T(8,128)(2,1)S(1)}, bf16[512,512]{1,0:T(8,128)(2,1)}, u32[]{:S(2)}) copy-start(bf16[512,512]{1,0:T(8,128)(2,1)} %constant.23.clone) | copy-start | bytes 1572868
  2.6 21.6 %all-to-all-start = ((bf16[16,4,32,256]{3,2,1,0:T(8,128)(2,1)}), bf16[16,4,32,256]{3,2,1,0:T(8,128)(2,1)}, u32[]{:S(2)}, u32[]{:S(2)}) async-start(bf16[16,4,32,256]{3,2,1,0:T(8,128)(2,1)} %bitcast.5), calls=%async_computation | async-start | bytes 2097152 | tf_op jit(solution)/shard_map/all_to_all | solution.py:263
  9.1 1.7 %copy-start.2 = (bf16[256,1024]{1,0:T(8,128)(2,1)S(1)}, bf16[256,1024]{1,0:T(8,128)(2,1)}, u32[]{:S(2)}) copy-start(bf16[256,1024]{1,0:T(8,128)(2,1)} %constant.24.clone) | copy-start | bytes 1572868
  9.1 1.7 %copy-start.6 = (f32[257]{0:T(512)S(1)}, f32[257]{0:T(512)}, u32[]{:S(2)}) copy-start(f32[257]{0:T(512)} %constant.32) | copy-start | bytes 3088
  10.8 1.0 copy-start.5
  11.6 1.0 copy-start.4
  11.8 1.1 copy-start
  74.1 2.7 %collective-permute-start = (bf16[1024,512]{1,0:T(8,128)(2,1)S(1)}, bf16[1024,512]{1,0:T(8,128)(2,1)S(1)}, u32[]{:S(2)}, u32[]{:S(2)}) collective-permute-start(bf16[1024,512]{1,0:T(8,128)(2,1)S(1)} %reshape.21.mine_ref), channel_id=1, source_target_pairs={{0,16},{16,0},{1,17},{17,1},{2,18},{18,2},{3,19},{19,3},{4,20},{20... | collective-permute-start | bytes 3145736 | tf_op jit(solution)/shard_map/ppermute | solution.py:285

commit v6 on v5

--- a/solution.py
+++ b/solution.py
@@ -29,6 +29,7 @@
 BF16 = jnp.bfloat16
 F8 = jnp.float8_e5m2
 SHIFT = 256.0
+LINE_SHIFT = 65536.0
 
 
 def split_table(table):
@@ -145,8 +146,8 @@
         line_im = jnp.where(first_row, jnp.broadcast_to(edge_line, (HALF, FAST)), line_im)
         packed = join([line_re, line_im], 1)
         upper = packed.astype(BF16)
-        lower = ((packed - upper.astype(F32)) * SHIFT).astype(F8)
-        mixed = dot(spread[...], upper) + dot(spread_lo[...], lower) * (1 / SHIFT)
+        lower = ((packed - upper.astype(F32)) * LINE_SHIFT).astype(F8)
+        mixed = dot(spread[...], upper) + dot(spread_lo[...], lower) * (1 / LINE_SHIFT)
         out_ref[:, 2 * FAST * column : 2 * FAST * (column + 1)] = mixed.astype(BF16)
 
 

time: 111 us -> 111 us (level)
  no operation moved by 1% of the time
where the time goes in v6:
time: 111 us
  blocking collectives  75.5 us (68%)
  waiting for transfers between devices  13.1 us (12%)
  Pallas kernels  8.04 us (7%)
  starting transfers between devices  6.49 us (6%)
  local copies, waits for them, and re-layouts  6.42 us (6%)
    all_to_all x3, blocking collectives, exchange(): return lax.all_to_all(values, axes, split_axis=0, concat_axis=0, tiled=True)  75.5 us
    all_to_all x1, waiting for transfers between devices, exchange(): return lax.all_to_all(values, axes, split_axis=0, concat_axis=0, tiled=True)  11.2 us
    all_to_all x1, starting transfers between devices, exchange(): return lax.all_to_all(values, axes, split_axis=0, concat_axis=0, tiled=True)  6.4 us
    pallas_call x1, Pallas kernels, filter_columns(): pl.pallas_call(filter_kernel, out_shape=jax.ShapeDtypeStruct((DEVICES, se...  5.54 us
    unnamed x26, local copies, waits for them, and re-layouts  4.72 us
  transfers between devices with their start and end apart: 2, of which 2 were waited for; matrix products, arithmetic and copies ran while one was open for 2% of the time, Pallas kernels for 1%

profile of v6, /device:TPU:8, one launch (start us, length us, event | category | flops | bytes accessed | tf_op | source)
XLA Modules:
  0.0 110.6 jit_solution(14327257650031770048)
XLA Ops:
  0.0 2.6 %copy.22 = bf16[8,8,32,256]{3,2,1,0:T(8,128)(2,1)} copy(bf16[8,8,32,256]{3,1,2,0:T(8,128)(2,1)} %bitcast.12) | data formatting | bytes 2097152
  2.6 6.4 %all-to-all-start = ((bf16[16,4,32,256]{3,2,1,0:T(8,128)(2,1)}), bf16[16,4,32,256]{3,2,1,0:T(8,128)(2,1)}, u32[]{:S(2)}, u32[]{:S(2)}) async-start(bf16[16,4,32,256]{3,2,1,0:T(8,128)(2,1)} %bitcast.5), calls=%async_computation | async-start | bytes 2097152 | tf_op jit(solution)/shard_map/all_to_all | solution.py:264
  9.0 0.1 reshape.19
  9.1 0.0 copy-start.2
  9.1 0.0 copy-start.6
  9.2 0.5 slice.27
  9.7 0.1 copy.18
  9.9 0.1 copy.21
  10.0 0.4 rev.6
  10.4 0.1 copy.20
  10.5 0.2 reverse.2
  10.7 0.1 slice.30
  10.8 0.0 copy-start.5
  10.8 0.8 fusion.1
  11.7 0.1 copy-done.5
  11.8 0.1 copy.36.table_ref
  11.9 0.8 copy-done.4
  12.7 0.1 copy.37.table_ref
  12.7 0.1 copy-done
  12.9 11.2 %all-to-all-done.series_ref = bf16[16,4,32,256]{3,2,1,0:T(8,128)(2,1)} async-done(((bf16[16,4,32,256]{3,2,1,0:T(8,128)(2,1)}), bf16[16,4,32,256]{3,2,1,0:T(8,128)(2,1)}, u32[]{:S(2)}, u32[]{:S(2)}) %all-to-all-start) | async-done | bytes 1048608 | tf_op jit(solution)/shard_map/all_to_all | solution.py:264
  24.1 5.5 %filter.1 = bf16[256,2048]{1,0:T(8,128)(2,1)S(1)} custom-call(bf16[16,4,32,256]{3,2,1,0:T(8,128)(2,1)} %all-to-all-done.series_ref, bf16[512,512]{1,0:T(8,128)(2,1)S(1)} %settle.5.fold_ref, bf16[256,1024]{1,0:T(8,128)(2,1)S(1)} %settle.6.inner_ref, f8e5m2[768,512]{1,0:T(32,128)(4,1)S(1)} %settle.7.coarse_ref, f8e5m2[512,768]{1,0:T(32,128)(4,1)S(1)} %settle.8.rest_ref, ...), custom_call_target="tpu_custom_call" | custom-call | flops 8000000000 | bytes 4194304 | tf_op jit(solution)/shard_map/filter/pallas_call | solution.py:155
  29.7 0.2 copy.23
  29.9 43.5 %all_to_all.20 = bf16[256,16,128]{2,1,0:T(8,128)(2,1)S(1)} all-to-all(bf16[256,16,128]{2,1,0:T(8,128)(2,1)S(1)} %bitcast.11), channel_id=1, replica_groups=mesh['yl'=2,'x'=4,'core'=2,'z'=8,'yh'=2] {'z','yh','yl','x','core'}, dimensions={0} | all-to-all | bytes 2097152 | tf_op jit(solution)/shard_map/all_to_all | solution.py:264
  73.4 0.6 reshape.21.mine_ref
  74.1 0.1 collective-permute-start
  74.2 0.7 gram_mine.1.begun_ref
  74.9 1.9 %collective-permute-done.other_ref = bf16[1024,512]{1,0:T(8,128)(2,1)S(1)} collective-permute-done((bf16[1024,512]{1,0:T(8,128)(2,1)S(1)}, bf16[1024,512]{1,0:T(8,128)(2,1)S(1)}, u32[]{:S(2)}, u32[]{:S(2)}) %collective-permute-start) | collective-permute-done | bytes 1048608 | tf_op jit(solution)/shard_map/ppermute | solution.py:286
  76.8 0.8 gram_other.1
  77.6 20.6 %all_to_all.21.parts_ref = bf16[16,64,512]{2,1,0:T(8,128)(2,1)S(1)} all-to-all(bf16[16,64,512]{2,1,0:T(8,128)(2,1)S(1)} %gram_other.1), channel_id=1, replica_groups=mesh['yl'=2,'x'=4,'core'=2,'z'=8,'yh'=2] {'yh','x','yl'}, dimensions={0} | all-to-all | bytes 2097152 | tf_op jit(solution)/shard_map/all_to_all | solution.py:264
  98.2 0.2 fold.1
  98.4 11.5 %all_to_all.22.parts_ref = f32[8,32,128]{2,1,0:T(8,128)S(1)} all-to-all(f32[8,32,128]{2,1,0:T(8,128)S(1)} %fold.1), channel_id=1, replica_groups=mesh['yl'=2,'x'=4,'core'=2,'z'=8,'yh'=2] {'z'}, dimensions={0} | all-to-all | bytes 262144 | tf_op jit(solution)/shard_map/all_to_all | solution.py:264
  109.8 0.8 finish.1
  (20 shorter events, 0.2 us)
Async XLA Ops:
  0.0 9.0 %copy-start.1 = (f32[131072]{0:T(1024)S(1)}, f32[131072]{0:T(1024)}, u32[]{:S(2)}) copy-start(f32[131072]{0:T(1024)} %param.9) | copy-start | bytes 1572868
  2.6 7.1 %copy-start.3 = (bf16[512,512]{1,0:T(8,128)(2,1)S(1)}, bf16[512,512]{1,0:T(8,128)(2,1)}, u32[]{:S(2)}) copy-start(bf16[512,512]{1,0:T(8,128)(2,1)} %constant.23.clone) | copy-start | bytes 1572868
  2.6 21.6 %all-to-all-start = ((bf16[16,4,32,256]{3,2,1,0:T(8,128)(2,1)}), bf16[16,4,32,256]{3,2,1,0:T(8,128)(2,1)}, u32[]{:S(2)}, u32[]{:S(2)}) async-start(bf16[16,4,32,256]{3,2,1,0:T(8,128)(2,1)} %bitcast.5), calls=%async_computation | async-start | bytes 2097152 | tf_op jit(solution)/shard_map/all_to_all | solution.py:264
  9.1 1.7 %copy-start.2 = (bf16[256,1024]{1,0:T(8,128)(2,1)S(1)}, bf16[256,1024]{1,0:T(8,128)(2,1)}, u32[]{:S(2)}) copy-start(bf16[256,1024]{1,0:T(8,128)(2,1)} %constant.24.clone) | copy-start | bytes 1572868
  9.1 1.7 %copy-start.6 = (f32[257]{0:T(512)S(1)}, f32[257]{0:T(512)}, u32[]{:S(2)}) copy-start(f32[257]{0:T(512)} %constant.32) | copy-start | bytes 3088
  10.8 1.0 copy-start.5
  11.6 1.0 copy-start.4
  11.8 1.1 copy-start
  74.1 2.7 %collective-permute-start = (bf16[1024,512]{1,0:T(8,128)(2,1)S(1)}, bf16[1024,512]{1,0:T(8,128)(2,1)S(1)}, u32[]{:S(2)}, u32[]{:S(2)}) collective-permute-start(bf16[1024,512]{1,0:T(8,128)(2,1)S(1)} %reshape.21.mine_ref), channel_id=1, source_target_pairs={{0,16},{16,0},{1,17},{17,1},{2,18},{18,2},{3,19},{19,3},{4,20},{20... | collective-permute-start | bytes 3145736 | tf_op jit(solution)/shard_map/ppermute | solution.py:286

commit v7 on v6

--- a/solution.py
+++ b/solution.py
@@ -210,14 +210,14 @@
     for pair in range(4):
         upper = total[0:32, pair * 128 : (pair + 1) * 128]
         lower = total[32:64, pair * 128 : (pair + 1) * 128]
-        out_ref[2 * pair] = jnp.where(lane, upper, pltpu.roll(lower, 64, 1))
-        out_ref[2 * pair + 1] = jnp.where(lane, pltpu.roll(upper, 64, 1), lower)
+        out_ref[2 * pair] = jnp.where(lane, upper, pltpu.roll(lower, 64, 1)).astype(BF16)
+        out_ref[2 * pair + 1] = jnp.where(lane, pltpu.roll(upper, 64, 1), lower).astype(BF16)
 
 
 def fold(parts):
     return pl.pallas_call(
         fold_kernel,
-        out_shape=jax.ShapeDtypeStruct((8, 32, 128), F32),
+        out_shape=jax.ShapeDtypeStruct((8, 32, 128), BF16),
         in_specs=[pl.BlockSpec(memory_space=pltpu.VMEM)],
         out_specs=pl.BlockSpec(memory_space=pltpu.VMEM),
         compiler_params=pltpu.CompilerParams(vmem_limit_bytes=FOLD_VMEM),
@@ -226,9 +226,9 @@
 
 
 def finish_kernel(parts_ref, out_ref):
-    total = parts_ref[0]
+    total = parts_ref[0].astype(F32)
     for part in range(1, parts_ref.shape[0]):
-        total += parts_ref[part]
+        total += parts_ref[part].astype(F32)
     block = join([total[:, 0:64], total[:, 64:128]], 0)
     out_ref[...] = block.T
 

time: 111 us -> 110 us (level)
  no operation moved by 1% of the time
where the time goes in v7:
time: 110 us
  blocking collectives  74.8 us (68%)
  waiting for transfers between devices  13.1 us (12%)
  Pallas kernels  8.04 us (7%)
  starting transfers between devices  6.49 us (6%)
  local copies, waits for them, and re-layouts  6.42 us (6%)
    all_to_all x3, blocking collectives, exchange(): return lax.all_to_all(values, axes, split_axis=0, concat_axis=0, tiled=True)  74.8 us
    all_to_all x1, waiting for transfers between devices, exchange(): return lax.all_to_all(values, axes, split_axis=0, concat_axis=0, tiled=True)  11.2 us
    all_to_all x1, starting transfers between devices, exchange(): return lax.all_to_all(values, axes, split_axis=0, concat_axis=0, tiled=True)  6.4 us
    pallas_call x1, Pallas kernels, filter_columns(): pl.pallas_call(filter_kernel, out_shape=jax.ShapeDtypeStruct((DEVICES, se...  5.54 us
    unnamed x26, local copies, waits for them, and re-layouts  4.72 us
  transfers between devices with their start and end apart: 2, of which 2 were waited for; matrix products, arithmetic and copies ran while one was open for 2% of the time, Pallas kernels for 1%

profile of v7, /device:TPU:8, one launch (start us, length us, event | category | flops | bytes accessed | tf_op | source)
XLA Modules:
  0.0 109.9 jit_solution(3560684777982455892)
XLA Ops:
  0.0 2.6 %copy.22 = bf16[8,8,32,256]{3,2,1,0:T(8,128)(2,1)} copy(bf16[8,8,32,256]{3,1,2,0:T(8,128)(2,1)} %bitcast.12) | data formatting | bytes 2097152
  2.6 6.4 %all-to-all-start = ((bf16[16,4,32,256]{3,2,1,0:T(8,128)(2,1)}), bf16[16,4,32,256]{3,2,1,0:T(8,128)(2,1)}, u32[]{:S(2)}, u32[]{:S(2)}) async-start(bf16[16,4,32,256]{3,2,1,0:T(8,128)(2,1)} %bitcast.5), calls=%async_computation | async-start | bytes 2097152 | tf_op jit(solution)/shard_map/all_to_all | solution.py:264
  9.0 0.1 reshape.19
  9.1 0.0 copy-start.2
  9.1 0.0 copy-start.6
  9.2 0.5 slice.27
  9.7 0.1 copy.18
  9.9 0.1 copy.21
  10.0 0.4 rev.6
  10.4 0.1 copy.20
  10.5 0.2 reverse.2
  10.7 0.1 slice.30
  10.8 0.0 copy-start.5
  10.8 0.8 fusion.1
  11.7 0.1 copy-done.5
  11.8 0.1 copy.36.table_ref
  11.9 0.8 copy-done.4
  12.7 0.1 copy.37.table_ref
  12.7 0.1 copy-done
  12.9 11.2 %all-to-all-done.series_ref = bf16[16,4,32,256]{3,2,1,0:T(8,128)(2,1)} async-done(((bf16[16,4,32,256]{3,2,1,0:T(8,128)(2,1)}), bf16[16,4,32,256]{3,2,1,0:T(8,128)(2,1)}, u32[]{:S(2)}, u32[]{:S(2)}) %all-to-all-start) | async-done | bytes 1048608 | tf_op jit(solution)/shard_map/all_to_all | solution.py:264
  24.1 5.5 %filter.1 = bf16[256,2048]{1,0:T(8,128)(2,1)S(1)} custom-call(bf16[16,4,32,256]{3,2,1,0:T(8,128)(2,1)} %all-to-all-done.series_ref, bf16[512,512]{1,0:T(8,128)(2,1)S(1)} %settle.5.fold_ref, bf16[256,1024]{1,0:T(8,128)(2,1)S(1)} %settle.6.inner_ref, f8e5m2[768,512]{1,0:T(32,128)(4,1)S(1)} %settle.7.coarse_ref, f8e5m2[512,768]{1,0:T(32,128)(4,1)S(1)} %settle.8.rest_ref, ...), custom_call_target="tpu_custom_call" | custom-call | flops 8000000000 | bytes 4194304 | tf_op jit(solution)/shard_map/filter/pallas_call | solution.py:155
  29.7 0.2 copy.23
  29.9 43.5 %all_to_all.20 = bf16[256,16,128]{2,1,0:T(8,128)(2,1)S(1)} all-to-all(bf16[256,16,128]{2,1,0:T(8,128)(2,1)S(1)} %bitcast.11), channel_id=1, replica_groups=mesh['yl'=2,'x'=4,'core'=2,'z'=8,'yh'=2] {'z','yh','yl','x','core'}, dimensions={0} | all-to-all | bytes 2097152 | tf_op jit(solution)/shard_map/all_to_all | solution.py:264
  73.4 0.6 reshape.21.mine_ref
  74.1 0.1 collective-permute-start
  74.2 0.7 gram_mine.1.begun_ref
  74.9 1.9 %collective-permute-done.other_ref = bf16[1024,512]{1,0:T(8,128)(2,1)S(1)} collective-permute-done((bf16[1024,512]{1,0:T(8,128)(2,1)S(1)}, bf16[1024,512]{1,0:T(8,128)(2,1)S(1)}, u32[]{:S(2)}, u32[]{:S(2)}) %collective-permute-start) | collective-permute-done | bytes 1048608 | tf_op jit(solution)/shard_map/ppermute | solution.py:286
  76.8 0.8 gram_other.1
  77.6 20.6 %all_to_all.21.parts_ref = bf16[16,64,512]{2,1,0:T(8,128)(2,1)S(1)} all-to-all(bf16[16,64,512]{2,1,0:T(8,128)(2,1)S(1)} %gram_other.1), channel_id=1, replica_groups=mesh['yl'=2,'x'=4,'core'=2,'z'=8,'yh'=2] {'yh','x','yl'}, dimensions={0} | all-to-all | bytes 2097152 | tf_op jit(solution)/shard_map/all_to_all | solution.py:264
  98.2 0.2 fold.1
  98.4 10.7 %all_to_all.22.parts_ref = bf16[8,32,128]{2,1,0:T(8,128)(2,1)S(1)} all-to-all(bf16[8,32,128]{2,1,0:T(8,128)(2,1)S(1)} %fold.1), channel_id=1, replica_groups=mesh['yl'=2,'x'=4,'core'=2,'z'=8,'yh'=2] {'z'}, dimensions={0} | all-to-all | bytes 131072 | tf_op jit(solution)/shard_map/all_to_all | solution.py:264
  109.1 0.8 finish.1
  (20 shorter events, 0.2 us)
Async XLA Ops:
  0.0 9.0 %copy-start.1 = (f32[131072]{0:T(1024)S(1)}, f32[131072]{0:T(1024)}, u32[]{:S(2)}) copy-start(f32[131072]{0:T(1024)} %param.9) | copy-start | bytes 1572868
  2.6 7.1 %copy-start.3 = (bf16[512,512]{1,0:T(8,128)(2,1)S(1)}, bf16[512,512]{1,0:T(8,128)(2,1)}, u32[]{:S(2)}) copy-start(bf16[512,512]{1,0:T(8,128)(2,1)} %constant.23.clone) | copy-start | bytes 1572868
  2.6 21.6 %all-to-all-start = ((bf16[16,4,32,256]{3,2,1,0:T(8,128)(2,1)}), bf16[16,4,32,256]{3,2,1,0:T(8,128)(2,1)}, u32[]{:S(2)}, u32[]{:S(2)}) async-start(bf16[16,4,32,256]{3,2,1,0:T(8,128)(2,1)} %bitcast.5), calls=%async_computation | async-start | bytes 2097152 | tf_op jit(solution)/shard_map/all_to_all | solution.py:264
  9.1 1.7 %copy-start.2 = (bf16[256,1024]{1,0:T(8,128)(2,1)S(1)}, bf16[256,1024]{1,0:T(8,128)(2,1)}, u32[]{:S(2)}) copy-start(bf16[256,1024]{1,0:T(8,128)(2,1)} %constant.24.clone) | copy-start | bytes 1572868
  9.1 1.7 %copy-start.6 = (f32[257]{0:T(512)S(1)}, f32[257]{0:T(512)}, u32[]{:S(2)}) copy-start(f32[257]{0:T(512)} %constant.32) | copy-start | bytes 3088
  10.8 1.0 copy-start.5
  11.6 1.0 copy-start.4
  11.8 1.1 copy-start
  74.1 2.7 %collective-permute-start = (bf16[1024,512]{1,0:T(8,128)(2,1)S(1)}, bf16[1024,512]{1,0:T(8,128)(2,1)S(1)}, u32[]{:S(2)}, u32[]{:S(2)}) collective-permute-start(bf16[1024,512]{1,0:T(8,128)(2,1)S(1)} %reshape.21.mine_ref), channel_id=1, source_target_pairs={{0,16},{16,0},{1,17},{17,1},{2,18},{18,2},{3,19},{19,3},{4,20},{20... | collective-permute-start | bytes 3145736 | tf_op jit(solution)/shard_map/ppermute | solution.py:286
